TPU v7x, 512 devices: a whole 4x8x8 slice. The times are simulated.
512 devices in a mesh: tp: 8 (over x, y_hi), seq: 64 (over z, y_lo, core).
Axes of the slice: x: 4, y: 8 (y_hi: 2, y_lo: 4; y = y_hi * 4 + y_lo), z: 8, core: 2. Of those that a mesh axis runs over, the one named last changes fastest.
Arguments:
- llama_context: bfloat16 [512, 4096], P(None, 'tp'), may hold values from -6 to 6
- llama_residual: bfloat16 [512, 4096], P(None, 'seq'), may hold values from -6 to 6
- w_attn_out: bfloat16 [4096, 4096], P('tp', 'seq'), may hold values from -0.09375 to 0.09375
- w_caption: bfloat16 [4096, 2560], P('seq', 'tp'), may hold values from -0.09375 to 0.09375
- w_text_kv: bfloat16 [2560, 2, 2048], P(None, None, 'tp'), may hold values from -0.125 to 0.125
- prompt_length: int32 [4], replicated, may hold values from 1 to 128, as said below
- image_query: bfloat16 [2, 16384, 2048], P(None, 'seq', 'tp'), may hold values from -32 to 32
- image_key: bfloat16 [2, 16384, 2048], P(None, 'seq', 'tp'), may hold values from -9 to 9
- image_value: bfloat16 [2, 16384, 2048], P(None, 'seq', 'tp'), may hold values from -6 to 6
Outputs:
- joint_context: bfloat16 [2, 16384, 2048], P(None, 'seq', 'tp')
Inputs may be any that keep to these rules, and one draw needn't show every extreme that they name: `prompt_length`: one pair's prompt has all 128 tokens live, every other pair's fewer.
All inputs are finite; a program needn't handle non-finite values.
Results may differ from a plain program's by a relative error of at most 0.039.
Values may be sent and summed in bfloat16 or wider, within the bound.
No kernel may reach another device: no remote copies, remote signals or barrier semaphores. Data moves between devices by JAX's collectives and lax.ppermute only.
A program may use at most 64 MiB of HBM per device.

v0:
```python
import math

import jax
import jax.numpy as jnp
from jax import lax
from jax.sharding import PartitionSpec as P

TXT = 128
HD = 128
IMG = 4096


def partner(value, axis, apart):
    mask = 2**apart
    pairs = [(source, source ^ mask) for source in range(lax.axis_size(axis))]
    return lax.ppermute(value, axis, pairs)


def local(
    llama_context,
    llama_residual,
    w_attn_out,
    w_caption,
    w_text_kv,
    prompt_length,
    image_query,
    image_key,
    image_value,
):
    llama_term = jnp.dot(llama_context, w_attn_out, preferred_element_type=jnp.float32)
    llama_attn = lax.psum(llama_term.astype(jnp.bfloat16), "tp").astype(jnp.float32)
    llama_hidden = (llama_residual.astype(jnp.float32) + llama_attn).astype(jnp.bfloat16)
    seq_index = lax.axis_index("seq")
    side_count, row_count, local_width = image_query.shape
    group_size = IMG // row_count
    text_rows = TXT // group_size
    caption_term = jnp.dot(llama_hidden, w_caption, preferred_element_type=jnp.float32)
    caption_whole = lax.psum(caption_term, "seq")
    text_part = lax.dynamic_slice_in_dim(caption_whole, seq_index * text_rows, text_rows, 0)
    text_states = lax.all_gather(text_part.astype(jnp.bfloat16), "tp", axis=1, tiled=True)
    text_kv = jnp.einsum(
        "td,djc->tjc", text_states, w_text_kv, preferred_element_type=jnp.float32
    ).astype(jnp.bfloat16)
    member = seq_index % group_size
    pair_index = seq_index // group_size
    pair_count = prompt_length.shape[0]
    live_length = jnp.sum(
        jnp.where(jnp.arange(pair_count, dtype=jnp.int32) == pair_index, prompt_length, 0)
    )
    text_place = member * text_rows + jnp.arange(text_rows, dtype=jnp.int32)
    text_bias = jnp.where(text_place < live_length, 0.0, -1e30).astype(jnp.bfloat16)
    local_heads = local_width // HD
    scale_factor = 1.0 / math.sqrt(HD)
    queries = image_query.reshape(side_count, row_count, local_heads, HD)

    def absorb(running, pieces):
        old_max, old_totals, old_accum = running
        text_piece, bias_piece, key_piece, value_piece = pieces
        text_count = text_piece.shape[0]
        piece_rows = key_piece.shape[1]
        text_keys = text_piece[:, 0].reshape(text_count, local_heads, HD)
        text_values = text_piece[:, 1].reshape(text_count, local_heads, HD)
        key_heads = key_piece.reshape(side_count, piece_rows, local_heads, HD)
        value_heads = value_piece.reshape(side_count, piece_rows, local_heads, HD)
        text_scores = (
            jnp.einsum("srhd,thd->shrt", queries, text_keys, preferred_element_type=jnp.float32)
            * scale_factor
        )
        text_scores = text_scores + bias_piece.astype(jnp.float32)[None, None, None, :]
        image_scores = (
            jnp.einsum("srhd,snhd->shrn", queries, key_heads, preferred_element_type=jnp.float32)
            * scale_factor
        )
        new_max = jnp.maximum(
            old_max, jnp.maximum(jnp.max(text_scores, axis=-1), jnp.max(image_scores, axis=-1))
        )
        factor = jnp.exp(old_max - new_max)
        text_weights = jnp.exp(text_scores - new_max[..., None])
        image_weights = jnp.exp(image_scores - new_max[..., None])
        new_totals = (
            old_totals * factor + jnp.sum(text_weights, axis=-1) + jnp.sum(image_weights, axis=-1)
        )
        addition = jnp.einsum(
            "shrt,thd->shrd",
            text_weights.astype(jnp.bfloat16),
            text_values,
            preferred_element_type=jnp.float32,
        )
        addition = addition + jnp.einsum(
            "shrn,snhd->shrd",
            image_weights.astype(jnp.bfloat16),
            value_heads,
            preferred_element_type=jnp.float32,
        )
        return (new_max, new_totals, old_accum * factor[..., None] + addition)

    start_max = jnp.full((side_count, local_heads, row_count), -1e30, jnp.float32)
    start_totals = jnp.zeros((side_count, local_heads, row_count), jnp.float32)
    start_accum = jnp.zeros((side_count, local_heads, row_count, HD), jnp.float32)
    collected = (text_kv, text_bias, image_key, image_value)
    running = absorb((start_max, start_totals, start_accum), collected)
    levels = group_size.bit_length() - 1
    bit_order = list(range(levels))
    for position, bit_number in enumerate(bit_order):
        arrived = partner(
            (collected[0], collected[1], collected[2], collected[3]), "seq", bit_number
        )
        running = absorb(running, arrived)
        if position + 1 < levels:
            collected = (
                jnp.concatenate((collected[0], arrived[0]), axis=0),
                jnp.concatenate((collected[1], arrived[1]), axis=0),
                jnp.concatenate((collected[2], arrived[2]), axis=1),
                jnp.concatenate((collected[3], arrived[3]), axis=1),
            )
    final_max, final_totals, final_accum = running
    context = (final_accum / final_totals[..., None]).astype(jnp.bfloat16)
    return context.transpose(0, 2, 1, 3).reshape(side_count, row_count, local_width)


def solution(mesh):
    placed = (
        P(None, "tp"),
        P(None, "seq"),
        P("tp", "seq"),
        P("seq", "tp"),
        P(None, None, "tp"),
        P(),
        P(None, "seq", "tp"),
        P(None, "seq", "tp"),
        P(None, "seq", "tp"),
    )
    return jax.shard_map(
        local, mesh=mesh, in_specs=placed, out_specs=P(None, "seq", "tp"), check_vma=False
    )
```

profile of v0, /device:TPU:1, one launch (start us, length us, event | category | flops | bytes accessed | tf_op | source)
XLA Modules:
  0.0 641.8 jit_solution(18367367319555831022)
XLA Ops:
  9.2 8.7 %collective-permute-start.1 = (bf16[8]{0:T(256)(128)(2,1)S(1)}, bf16[8]{0:T(256)(128)(2,1)S(1)}, u32[]{:S(2)}, u32[]{:S(2)}) collective-permute-start(bf16[8]{0:T(256)(128)(2,1)S(1)} %get-tuple-element.18), channel_id=1, source_target_pairs={{0,1},{1,0},{2,3},{3,2},{4,5},{5,4},{6,7},{7,6},{8,9},{9,8},{10,11... | collective-permute-start | bytes 56 | tf_op jit(solution)/shard_map/ppermute | solution.py:16
  17.9 2.0 convolution_convert_fusion
  21.0 1.9 collective-permute-start.2
  24.7 2.4 collective-permute-start.3
  27.1 2.9 fusion.150
  30.1 1.9 collective-permute-start.5
  32.0 2.4 collective-permute-done.5
  34.5 1.9 collective-permute-start.9
  36.9 2.7 collective-permute-done.9
  39.7 1.9 collective-permute-start.13
  44.6 79.9 %all-reduce.3.cloned.1.call-done = bf16[512,64]{0,1:T(8,128)(2,1)} async-done(((bf16[512,64]{0,1:T(8,128)(2,1)}), bf16[512,64]{0,1:T(8,128)(2,1)}) %all-reduce.3.cloned.1.call-update) | async-done | bytes 65552 | tf_op jit(solution)/shard_map/psum | solution.py:31
  124.6 2.0 fusion.97
  126.6 272.4 %all-reduce.4 = bf16[512,320]{1,0:T(8,128)(2,1)} all-reduce(f32[512,320]{1,0:T(8,128)} %fusion.97), channel_id=1, replica_groups=mesh['tp'=8,'seq'=64] {'seq'}, use_global_device_ids=true, to_apply=%region_1.0 | all-reduce | flops 163840 | bytes 983040 | tf_op jit(solution)/shard_map/psum | solution.py:38
  399.6 37.7 %all-gather = bf16[8,320,8]{1,2,0:T(8,128)(2,1)S(1)} all-gather(bf16[1,320,8]{1,2,0:T(8,128)(2,1)S(1)} %fusion.117), channel_id=1, replica_groups=mesh['tp'=8,'seq'=64] {'tp'}, dimensions={0}, use_global_device_ids=true | all-gather | bytes 46080 | tf_op jit(solution)/shard_map/all_gather | solution.py:40
  437.9 14.5 %collective-permute-start = (bf16[8,2,256]{2,0,1:T(8,128)(2,1)S(1)}, bf16[8,2,256]{2,0,1:T(8,128)(2,1)S(1)}, u32[]{:S(2)}, u32[]{:S(2)}) collective-permute-start(bf16[8,2,256]{2,0,1:T(8,128)(2,1)S(1)} %fusion.50), channel_id=1, source_target_pairs={{0,1},{1,0},{2,3},{3,2},{4,5},{5,4},{6,7},{7,6},{8,9},{9,8},{10,11... | collective-permute-start | bytes 24584 | tf_op jit(solution)/shard_map/ppermute | solution.py:16
  453.2 1.9 collective-permute-start.4
  456.7 3.3 collective-permute-start.6
  461.5 1.9 collective-permute-start.8
  464.6 8.0 %collective-permute-done.6 = bf16[2,512,256]{1,2,0:T(8,128)(2,1)S(1)} collective-permute-done((bf16[2,512,256]{1,2,0:T(8,128)(2,1)}, bf16[2,512,256]{1,2,0:T(8,128)(2,1)S(1)}, u32[]{:S(2)}, u32[]{:S(2)}) %collective-permute-start.6) | collective-permute-done | bytes 524320 | tf_op jit(solution)/shard_map/ppermute | solution.py:16
  472.6 2.2 pad_maximum_fusion.2
  474.8 1.9 collective-permute-start.10
  480.9 1.9 collective-permute-start.12
  486.8 2.2 fusion.145
  490.8 2.4 collective-permute-start.7
  496.0 29.3 %collective-permute-done.10 = bf16[2,1024,256]{1,2,0:T(8,128)(2,1)} collective-permute-done((bf16[2,1024,256]{1,2,0:T(8,128)(2,1)}, bf16[2,1024,256]{1,2,0:T(8,128)(2,1)}, u32[]{:S(2)}, u32[]{:S(2)}) %collective-permute-start.10) | collective-permute-done | bytes 1048608 | tf_op jit(solution)/shard_map/ppermute | solution.py:16
  525.3 3.0 pad_maximum_fusion
  534.5 1.9 collective-permute-start.11
  538.1 44.0 %collective-permute-done.11 = bf16[2,1024,256]{1,2,0:T(8,128)(2,1)S(1)} collective-permute-done((bf16[2,1024,256]{1,2,0:T(8,128)(2,1)S(1)}, bf16[2,1024,256]{1,2,0:T(8,128)(2,1)S(1)}, u32[]{:S(2)}, u32[]{:S(2)}) %collective-permute-start.11) | collective-permute-done | bytes 1048608 | tf_op jit(solution)/shard_map/ppermute | solution.py:16
  583.5 3.5 collective-permute-start.15
  587.1 2.0 bitcast_reduce_fusion.1
  589.1 3.0 bitcast_reduce_fusion
  598.7 33.4 %collective-permute-done.15 = bf16[2,2048,256]{1,2,0:T(8,128)(2,1)S(1)} collective-permute-done((bf16[2,2048,256]{1,2,0:T(8,128)(2,1)S(1)}, bf16[2,2048,256]{1,2,0:T(8,128)(2,1)S(1)}, u32[]{:S(2)}, u32[]{:S(2)}) %collective-permute-start.15) | collective-permute-done | bytes 2097184 | tf_op jit(solution)/shard_map/ppermute | solution.py:16
  (131 shorter events, 46.6 us)
Async XLA Ops:
  6.5 430.9 %copy-start = (bf16[2560,2,256]{2,1,0:T(2,128)(2,1)S(1)}, bf16[2560,2,256]{2,1,0:T(2,128)(2,1)}, u32[]{:S(2)}) copy-start(bf16[2560,2,256]{2,1,0:T(2,128)(2,1)} %param.13) | copy-start | bytes 7864324
  6.5 118.0 %copy-start.12 = (bf16[512,64]{0,1:T(8,128)(2,1)S(1)}, bf16[512,64]{0,1:T(8,128)(2,1)}, u32[]{:S(2)}) copy-start(bf16[512,64]{0,1:T(8,128)(2,1)} %param.10) | copy-start | bytes 196612
  6.5 118.0 %copy-start.13 = (bf16[64,320]{1,0:T(8,128)(2,1)S(1)}, bf16[64,320]{1,0:T(8,128)(2,1)}, u32[]{:S(2)}) copy-start(bf16[64,320]{1,0:T(8,128)(2,1)} %param.12) | copy-start | bytes 122884
  6.5 118.0 %all-reduce.3.cloned.1.call-start = ((), (), s32[]{:S(2)}) async-start(), calls=%async_computation | async-start | bytes 131072 | tf_op jit(solution)/shard_map/psum | solution.py:31
  9.2 20.8 %collective-permute-start.1 = (bf16[8]{0:T(256)(128)(2,1)S(1)}, bf16[8]{0:T(256)(128)(2,1)S(1)}, u32[]{:S(2)}, u32[]{:S(2)}) collective-permute-start(bf16[8]{0:T(256)(128)(2,1)S(1)} %get-tuple-element.18), channel_id=1, source_target_pairs={{0,1},{1,0},{2,3},{3,2},{4,5},{5,4},{6,7},{7,6},{8,9},{9,8},{10,11... | collective-permute-start | bytes 56 | tf_op jit(solution)/shard_map/ppermute | solution.py:16
  21.0 434.2 %copy-start.3 = (bf16[2,256,256]{1,2,0:T(8,128)(2,1)}, bf16[2,256,256]{1,2,0:T(8,128)(2,1)S(1)}, u32[]{:S(2)}) copy-start(bf16[2,256,256]{1,2,0:T(8,128)(2,1)S(1)} %copy.207) | copy-start | bytes 786436
  21.0 434.2 %collective-permute-start.2 = (bf16[2,256,256]{1,2,0:T(8,128)(2,1)S(1)}, bf16[2,256,256]{1,2,0:T(8,128)(2,1)S(1)}, u32[]{:S(2)}, u32[]{:S(2)}) collective-permute-start(bf16[2,256,256]{1,2,0:T(8,128)(2,1)S(1)} %copy.207), channel_id=1, source_target_pairs={{0,1},{1,0},{2,3},{3,2},{4,5},{5,4},{6,7},{7,6},{8,9},{9,8},{10,11... | collective-permute-start | bytes 786440 | tf_op jit(solution)/shard_map/ppermute | solution.py:16
  24.7 464.2 %collective-permute-start.3 = (bf16[2,256,256]{1,2,0:T(8,128)(2,1)}, bf16[2,256,256]{1,2,0:T(8,128)(2,1)}, u32[]{:S(2)}, u32[]{:S(2)}) collective-permute-start(bf16[2,256,256]{1,2,0:T(8,128)(2,1)} %copy.212), channel_id=1, source_target_pairs={{0,1},{1,0},{2,3},{3,2},{4,5},{5,4},{6,7},{7,6},{8,9},{9,8},{10,11... | collective-permute-start | bytes 786440 | tf_op jit(solution)/shard_map/ppermute | solution.py:16
  30.1 4.3 collective-permute-start.5
  34.5 5.2 collective-permute-start.9
  39.7 4.3 collective-permute-start.13
  126.6 325.9 %copy-start.1 = (bf16[2,256,256]{2,1,0:T(8,128)(2,1)S(1)}, bf16[2,256,256]{2,1,0:T(8,128)(2,1)}, u32[]{:S(2)}) copy-start(bf16[2,256,256]{2,1,0:T(8,128)(2,1)} %param.15) | copy-start | bytes 786436
  126.6 325.9 %copy-start.23 = (f32[8]{0:T(128)S(1)}, f32[8]{0:T(128)}, u32[]{:S(2)}) copy-start(f32[8]{0:T(128)} %get-tuple-element.17) | copy-start | bytes 100
  437.4 22.7 %copy-start.25 = (f32[8]{0:T(128)S(1)}, f32[8]{0:T(128)}, u32[]{:S(2)}) copy-start(f32[8]{0:T(128)} %convert_element_type.88) | copy-start | bytes 100
  437.9 15.3 %collective-permute-start = (bf16[8,2,256]{2,0,1:T(8,128)(2,1)S(1)}, bf16[8,2,256]{2,0,1:T(8,128)(2,1)S(1)}, u32[]{:S(2)}, u32[]{:S(2)}) collective-permute-start(bf16[8,2,256]{2,0,1:T(8,128)(2,1)S(1)} %fusion.50), channel_id=1, source_target_pairs={{0,1},{1,0},{2,3},{3,2},{4,5},{5,4},{6,7},{7,6},{8,9},{9,8},{10,11... | collective-permute-start | bytes 24584 | tf_op jit(solution)/shard_map/ppermute | solution.py:16
  453.2 7.6 %collective-permute-start.4 = (bf16[16,2,256]{2,0,1:T(8,128)(2,1)S(1)}, bf16[16,2,256]{2,0,1:T(8,128)(2,1)S(1)}, u32[]{:S(2)}, u32[]{:S(2)}) collective-permute-start(bf16[16,2,256]{2,0,1:T(8,128)(2,1)S(1)} %pad_maximum_fusion.8), channel_id=1, source_target_pairs={{0,2},{1,3},{2,0},{3,1},{4,6},{5,7},{6,4},{7,5},{8,10},{9,11},{10,... | collective-permute-start | bytes 49160 | tf_op jit(solution)/shard_map/ppermute | solution.py:16
  456.7 15.9 %collective-permute-start.6 = (bf16[2,512,256]{1,2,0:T(8,128)(2,1)}, bf16[2,512,256]{1,2,0:T(8,128)(2,1)S(1)}, u32[]{:S(2)}, u32[]{:S(2)}) collective-permute-start(bf16[2,512,256]{1,2,0:T(8,128)(2,1)} %pad_maximum_fusion.4), channel_id=1, source_target_pairs={{0,2},{1,3},{2,0},{3,1},{4,6},{5,7},{6,4},{7,5},{8,10},{9,11},{10,... | collective-permute-start | bytes 1572872 | tf_op jit(solution)/shard_map/ppermute | solution.py:16
  461.5 18.0 %collective-permute-start.8 = (bf16[32,2,256]{2,0,1:T(8,128)(2,1)}, bf16[32,2,256]{2,0,1:T(8,128)(2,1)}, u32[]{:S(2)}, u32[]{:S(2)}) collective-permute-start(bf16[32,2,256]{2,0,1:T(8,128)(2,1)} %pad_maximum_fusion.7), channel_id=1, source_target_pairs={{0,4},{1,5},{2,6},{3,7},{4,0},{5,1},{6,2},{7,3},{8,12},{9,13},{10,... | collective-permute-start | bytes 98312 | tf_op jit(solution)/shard_map/ppermute | solution.py:16
  464.6 12.1 %copy-start.19 = (bf16[16,2,128]{2,1,0:T(2,128)(2,1)S(1)}, bf16[16,2,128]{2,1,0:T(2,128)(2,1)}, u32[]{:S(2)}) copy-start(bf16[16,2,128]{2,1,0:T(2,128)(2,1)} %reshape_squeeze.34) | copy-start | bytes 24580
  474.8 50.5 %collective-permute-start.10 = (bf16[2,1024,256]{1,2,0:T(8,128)(2,1)}, bf16[2,1024,256]{1,2,0:T(8,128)(2,1)}, u32[]{:S(2)}, u32[]{:S(2)}) collective-permute-start(bf16[2,1024,256]{1,2,0:T(8,128)(2,1)} %pad_maximum_fusion.2), channel_id=1, source_target_pairs={{0,4},{1,5},{2,6},{3,7},{4,0},{5,1},{6,2},{7,3},{8,12},{9,13},{10,... | collective-permute-start | bytes 3145736 | tf_op jit(solution)/shard_map/ppermute | solution.py:16
  480.9 12.3 %collective-permute-start.12 = (bf16[64,2,256]{2,0,1:T(8,128)(2,1)}, bf16[64,2,256]{2,0,1:T(8,128)(2,1)}, u32[]{:S(2)}, u32[]{:S(2)}) collective-permute-start(bf16[64,2,256]{2,0,1:T(8,128)(2,1)} %pad_maximum_fusion.6), channel_id=1, source_target_pairs={{0,8},{1,9},{2,10},{3,11},{4,12},{5,13},{6,14},{7,15},{8,0},{9,1},... | collective-permute-start | bytes 196616 | tf_op jit(solution)/shard_map/ppermute | solution.py:16
  490.8 42.3 %collective-permute-start.7 = (bf16[2,512,256]{1,2,0:T(8,128)(2,1)}, bf16[2,512,256]{1,2,0:T(8,128)(2,1)}, u32[]{:S(2)}, u32[]{:S(2)}) collective-permute-start(bf16[2,512,256]{1,2,0:T(8,128)(2,1)} %pad_maximum_fusion.5), channel_id=1, source_target_pairs={{0,2},{1,3},{2,0},{3,1},{4,6},{5,7},{6,4},{7,5},{8,10},{9,11},{10,... | collective-permute-start | bytes 1572872 | tf_op jit(solution)/shard_map/ppermute | solution.py:16
  496.0 34.2 %copy-start.10 = (bf16[64,2,128]{2,1,0:T(2,128)(2,1)S(1)}, bf16[64,2,128]{2,1,0:T(2,128)(2,1)}, u32[]{:S(2)}) copy-start(bf16[64,2,128]{2,1,0:T(2,128)(2,1)} %reshape_squeeze.38) | copy-start | bytes 98308
  496.0 34.2 %copy-start.24 = (f32[64]{0:T(128)S(1)}, f32[64]{0:T(128)}, u32[]{:S(2)}) copy-start(f32[64]{0:T(128)} %convert_element_type.97) | copy-start | bytes 772
  528.3 60.8 %collective-permute-start.14 = (bf16[2,2048,256]{1,2,0:T(8,128)(2,1)}, bf16[2,2048,256]{1,2,0:T(8,128)(2,1)}, u32[]{:S(2)}, u32[]{:S(2)}) collective-permute-start(bf16[2,2048,256]{1,2,0:T(8,128)(2,1)} %pad_maximum_fusion), channel_id=1, source_target_pairs={{0,8},{1,9},{2,10},{3,11},{4,12},{5,13},{6,14},{7,15},{8,0},{9,1},... | collective-permute-start | bytes 6291464 | tf_op jit(solution)/shard_map/ppermute | solution.py:16
  533.1 3.3 copy-start.5
  534.5 47.7 %collective-permute-start.11 = (bf16[2,1024,256]{1,2,0:T(8,128)(2,1)S(1)}, bf16[2,1024,256]{1,2,0:T(8,128)(2,1)S(1)}, u32[]{:S(2)}, u32[]{:S(2)}) collective-permute-start(bf16[2,1024,256]{1,2,0:T(8,128)(2,1)S(1)} %pad_maximum_fusion.3), channel_id=1, source_target_pairs={{0,4},{1,5},{2,6},{3,7},{4,0},{5,1},{6,2},{7,3},{8,12},{9,13},{10,... | collective-permute-start | bytes 3145736 | tf_op jit(solution)/shard_map/ppermute | solution.py:16
  583.5 48.6 %collective-permute-start.15 = (bf16[2,2048,256]{1,2,0:T(8,128)(2,1)S(1)}, bf16[2,2048,256]{1,2,0:T(8,128)(2,1)S(1)}, u32[]{:S(2)}, u32[]{:S(2)}) collective-permute-start(bf16[2,2048,256]{1,2,0:T(8,128)(2,1)S(1)} %pad_maximum_fusion.1), channel_id=1, source_target_pairs={{0,8},{1,9},{2,10},{3,11},{4,12},{5,13},{6,14},{7,15},{8,0},{9,1},... | collective-permute-start | bytes 6291464 | tf_op jit(solution)/shard_map/ppermute | solution.py:16
  589.1 3.0 copy-start.14
  589.1 3.0 copy-start.16
  589.1 3.0 copy-start.6
  589.1 3.1 copy-start.8
  (11 other events, 12.7 us)
Sparse Core Ops, SparseCore 0:
  20.0 104.4 all-reduce.2
where the time goes:
time: 644 us; the launch traced here: 642 us
  blocking collectives  310 us (48%)
  waiting for transfers between devices  201 us (31%)
  starting transfers between devices  54 us (8%)
  matrix products  25.1 us (4%)
  other arithmetic  21.1 us (3%)
  local copies, waits for them, and re-layouts  16.3 us (3%)
  between operations  14.1 us (2%)
    psum x1, blocking collectives, local(): caption_whole = lax.psum(caption_term, 'seq')  272 us
    ppermute x16, waiting for transfers between devices, partner(): return lax.ppermute(value, axis, pairs)  121 us
    psum x1, waiting for transfers between devices, local(): lax.psum(llama_term.astype(jnp.bfloat16), 'tp').astype(jnp.float32)  79.9 us
    ppermute x16, starting transfers between devices, partner(): return lax.ppermute(value, axis, pairs)  54 us
    all_gather x1, blocking collectives, local(): lax.all_gather(text_part.astype(jnp.bfloat16), 'tp', axis=1, tiled=True)  37.7 us
  transfers between devices with their start and end apart: 17, of which 8 were waited for; matrix products, arithmetic and copies ran while one was open for 9% of the time, Pallas kernels for 0%

commit v1 on v0

v1 whole, which is shorter than its diff:
```python
import math

import jax
import jax.numpy as jnp
from jax import lax
from jax.experimental import pallas as pl
from jax.experimental.pallas import tpu as pltpu
from jax.sharding import PartitionSpec as P


TXT = 128
HD = 128
NEG = -1e30
BF = jnp.bfloat16
F32 = jnp.float32
SCALE = 1.0 / math.sqrt(HD)
LOG2E = math.log2(math.e)

X, Z_HI, GROUP = 4, 4, 16
CAP = 384
NT = (((1,), (1,)), ((), ()))
TN = (((0,), (0,)), ((), ()))


def spread(value):
    groups = [[p * GROUP + m for m in range(GROUP)] for p in range(Z_HI)]
    return lax.all_to_all(value, "seq", 0, 0, axis_index_groups=groups)


def shifted(value, axis, span, stride, step):
    size = lax.axis_size(axis)
    to = lambda i: i + ((i // stride % span + step) % span - i // stride % span) * stride
    return lax.ppermute(value, axis, [(i, to(i)) for i in range(size)])


KEYS, PIECE = TXT, 64
SENT = 2 * KEYS + PIECE
LSE, TEXT = PIECE, PIECE + 8
BACK = TEXT + 32


def duty(m):
    return m // 8, m // 2 % 2, m % 2, m // 4 % 2 * 2 + m % 2


def call(kernel, args, outs, scalars=0, mib=4, **extra):
    vmem = pl.BlockSpec(memory_space=pltpu.VMEM)
    smem = pl.BlockSpec(memory_space=pltpu.SMEM)
    result = pl.pallas_call(
        kernel,
        in_specs=[smem] * scalars + [vmem] * (len(args) - scalars),
        out_specs=[vmem] * len(outs),
        out_shape=outs,
        compiler_params=pltpu.CompilerParams(vmem_limit_bytes=mib << 20),
        **extra,
    )(*args)
    return result[0] if len(outs) == 1 else result


def after(value, *others):
    return lax.optimization_barrier((value, *others))[0]


def shape(*dims, dtype=BF):
    return jax.ShapeDtypeStruct(dims, dtype)


def project_kernel(ctx_ref, w_ref, cap_ref, out_ref):
    term = lax.dot_general(w_ref[...], ctx_ref[...], NT, preferred_element_type=F32)
    rows = term.shape[1]
    out_ref[:, :rows] = term.astype(BF)
    out_ref[:, rows : rows + cap_ref.shape[1]] = cap_ref[...]
    out_ref[:, rows + cap_ref.shape[1] :] = jnp.zeros_like(out_ref[:, rows + cap_ref.shape[1] :])


def near_kernel(own_ref, far_ref, out_ref):
    rows = own_ref.shape[1] - CAP
    out_ref[:, :rows] = (own_ref[:, :rows].astype(F32) + far_ref[:, :rows].astype(F32)).astype(BF)
    out_ref[:, rows : rows + CAP] = own_ref[:, rows:]
    out_ref[:, rows + CAP :] = far_ref[:, rows:]


def joint_kernel(pos_ref, n0, n1, n2, n3, res_ref, w_ref, o0, o1, o2, o3, hid_ref):
    x, yhi, zhi = pos_ref[0], pos_ref[1], pos_ref[2]
    rows = hid_ref.shape[1]
    cols = w_ref.shape[0] // (2 * X)
    total = res_ref[...].astype(F32)
    joint = jnp.zeros((total.shape[0], w_ref.shape[1]), F32)
    for step, ref in enumerate((n0, n1, n2, n3)):
        total = total + ref[:, :rows].astype(F32)
        source = (x + X - step) % X
        for far in range(2):
            block = source * 2 + (yhi + far) % 2
            first = pl.multiple_of(block * cols, cols)
            cap = ref[:, rows + far * CAP : rows + far * CAP + cols]
            joint += jnp.dot(cap, w_ref[pl.ds(first, cols), :], preferred_element_type=F32)
    hid_ref[...] = total.astype(BF)
    joint = joint.astype(BF)
    for step, ref in enumerate((o0, o1, o2, o3)):
        first = pl.multiple_of((zhi + step) % Z_HI * TXT, TXT)
        ref[:, :TXT] = hid_ref[:, pl.ds(first, TXT)]
        ref[:, TXT:] = joint


def part_kernel(g0, g1, g2, g3, out_ref):
    part = None
    for ref in (g0, g1, g2, g3):
        term = lax.dot_general(ref[:, :TXT], ref[:, TXT:], TN, preferred_element_type=F32)
        part = term if part is None else part + term
    out_ref[...] = part.astype(BF).reshape(out_ref.shape)


def sum_kernel(part_ref, o_ref, out_ref):
    total = jnp.sum(part_ref[...].astype(F32), axis=0)
    text = jnp.concatenate([total[:, i * HD : (i + 1) * HD] for i in range(4)], axis=0).astype(BF)
    for m in range(GROUP):
        out_ref[m, :TEXT] = o_ref[m]
        out_ref[m, TEXT:] = text


def pack_kernel(_, k_ref, v_ref, q_ref, out_ref):
    for m in range(GROUP):
        side, head, keys, piece = duty(m)
        cols = slice(head * HD, (head + 1) * HD)
        out_ref[m, :KEYS] = k_ref[side, keys * KEYS : (keys + 1) * KEYS, cols]
        out_ref[m, KEYS : 2 * KEYS] = v_ref[side, keys * KEYS : (keys + 1) * KEYS, cols]
        out_ref[m, 2 * KEYS :] = q_ref[side, piece * PIECE : (piece + 1) * PIECE, cols]


def image_kernel(own_ref, other_ref, out_ref):
    for block in range(4):
        members = slice(block * 4, block * 4 + 4)
        q = own_ref[members, 2 * KEYS :].reshape(-1, HD)
        s = [
            lax.dot_general(q, ref[:, :KEYS].reshape(-1, HD), NT, preferred_element_type=F32)
            for ref in (own_ref, other_ref)
        ]
        top = jnp.maximum(*(jnp.max(t, axis=1, keepdims=True) for t in s))
        p = [jnp.exp2(t * (SCALE * LOG2E) - top * (SCALE * LOG2E)) for t in s]
        total = sum(jnp.sum(t, axis=1, keepdims=True) for t in p)
        acc = sum(
            jnp.dot(t.astype(BF), ref[:, KEYS : 2 * KEYS].reshape(-1, HD), preferred_element_type=F32)
            for t, ref in zip(p, (own_ref, other_ref), strict=True)
        )
        out_ref[members, :PIECE] = (acc / total).astype(BF).reshape(4, PIECE, HD)
        rest = top * SCALE + jnp.log(total)
        rest = jnp.transpose(jnp.broadcast_to(rest, (q.shape[0], HD)))[:8]
        first = rest.astype(BF).astype(F32)
        rest = rest - first
        second = rest.astype(BF).astype(F32)
        place = lax.broadcasted_iota(jnp.int32, rest.shape, 0)
        lse = jnp.where(place == 0, first, jnp.where(place == 1, second, rest - second))
        for i in range(4):
            row = jnp.concatenate([lse[:, i * PIECE : (i + 1) * PIECE]] * 2, axis=1)
            out_ref[block * 4 + i, LSE:TEXT] = row.astype(BF)


def text_kernel(pair_ref, live_ref, q_ref, back_ref, out_ref):
    live = live_ref[pair_ref[0]]
    text = [
        back_ref[:, TEXT + 8 * i : TEXT + 8 * i + 8].astype(F32).reshape(TXT, HD).astype(BF) for i in range(4)
    ]
    kept = lax.broadcasted_iota(jnp.int32, (PIECE, TXT), 1) < live
    for m in range(GROUP):
        side, head, _, piece = duty(m)
        place = (side, slice(piece * PIECE, (piece + 1) * PIECE), slice(head * HD, (head + 1) * HD))
        s = lax.dot_general(q_ref[place], text[head], NT, preferred_element_type=F32) * SCALE
        s = jnp.where(kept, s, NEG)
        tail = back_ref[m, LSE:TEXT].astype(F32)
        lse = jnp.broadcast_to(tail[:1] + tail[1:2] + tail[2:3], tail.shape)
        lse = jnp.transpose(lse)[:PIECE, :1]
        top = jnp.maximum(jnp.max(s, axis=1, keepdims=True), lse)
        p = jnp.exp(s - top)
        image = jnp.exp(lse - top)
        total = image + jnp.sum(p, axis=1, keepdims=True)
        acc = jnp.dot(p.astype(BF), text[2 + head], preferred_element_type=F32)
        acc += image * back_ref[m, :PIECE].astype(F32)
        out_ref[place] = (acc / total).astype(BF)


def local(
    llama_context,
    llama_residual,
    w_attn_out,
    w_caption,
    w_text_kv,
    prompt_length,
    image_query,
    image_key,
    image_value,
):
    tp, seq = lax.axis_index("tp"), lax.axis_index("seq")
    pos = jnp.stack((tp >> 1, tp & 1, seq >> 4))
    feats, text_rows = w_attn_out.shape[1], llama_context.shape[0]
    w_kv = w_text_kv.reshape(w_text_kv.shape[0], -1)
    kv_cols = w_kv.shape[1]

    term = call(project_kernel, (llama_context, w_attn_out.T, w_caption), [shape(feats, text_rows + CAP)])
    far = lax.ppermute(term, "tp", [(t, t ^ 1) for t in range(2 * X)])
    own = call(pack_kernel, (term, image_key, image_value, image_query), [shape(GROUP, SENT, HD)])
    own = spread(own)

    near = call(near_kernel, (term, far), [shape(feats, text_rows + 2 * CAP)])
    ring = [near] + [shifted(near, "tp", X, 2, step) for step in range(1, X)]
    sends = call(
        joint_kernel,
        (pos, *ring, llama_residual.T, w_kv),
        [shape(feats, TXT + kv_cols)] * Z_HI,
        scalars=1,
        mib=8,
        scratch_shapes=[pltpu.VMEM((feats, text_rows), BF)],
    )
    parts = [sends[0]] + [shifted(sends[step], "seq", Z_HI, GROUP, step) for step in range(1, Z_HI)]
    part = call(part_kernel, parts, [shape(GROUP, TXT // GROUP, kv_cols)])

    part, own = lax.optimization_barrier((part, own))
    other = lax.ppermute(own, "seq", [(i, i ^ 1) for i in range(Z_HI * GROUP)])
    part = spread(part)
    o = call(image_kernel, (own, other), [shape(GROUP, TEXT, HD)], mib=32)
    back = call(sum_kernel, (after(part, o), o), [shape(GROUP, BACK, HD)])
    back = spread(back)
    return call(text_kernel, (pos[2:], prompt_length, image_query, back), [shape(*image_query.shape)], scalars=2)


def solution(mesh):
    placed = (
        P(None, "tp"),
        P(None, "seq"),
        P("tp", "seq"),
        P("seq", "tp"),
        P(None, None, "tp"),
        P(),
        P(None, "seq", "tp"),
        P(None, "seq", "tp"),
        P(None, "seq", "tp"),
    )

    return jax.shard_map(local, mesh=mesh, in_specs=placed, out_specs=P(None, "seq", "tp"), check_vma=False)
```

time: 644 us -> 130 us (0.20)
  blocking collectives: 310 us -> 18.3 us
  waiting for transfers between devices: 201 us -> 31.3 us
  matrix products: 25.1 us -> 0 us
  other arithmetic: 21.1 us -> 0.08 us
  Pallas kernels: 0 us -> 19.7 us
  between operations: 14.1 us -> 0.15 us
  local copies, waits for them, and re-layouts: 16.3 us -> 7.77 us
    psum x1 -> x0, blocking collectives: 272 us -> none  [local(): caption_whole = lax.psum(caption_term, 'seq')]
    ppermute x16 -> x8, waiting for transfers between devices: 121 us -> 31.3 us  [the longest x1 25.7 us: local(): far = lax.ppermute(term, 'tp', [(t, t ^ 1) for t in range(2 * X)])]
    psum x1 -> x0, waiting for transfers between devices: 79.9 us -> none  [local(): lax.psum(llama_term.astype(jnp.bfloat16), 'tp').astype(jnp.float32)]
    all_gather x1 -> x0, blocking collectives: 37.7 us -> none  [local(): lax.all_gather(text_part.astype(jnp.bfloat16), 'tp', axis=1, tiled=True)]
    dot_general x23 -> x0, matrix products: 25.1 us -> none  [the longest x5 8.71 us: absorb(): jnp.einsum('srhd,snhd->shrn', queries, key_heads, preferred_element_type=...]
    pallas_call x0 -> x8, Pallas kernels: none -> 19.7 us  [call(): pl.pallas_call(kernel, in_specs=[smem] * scalars + [vmem] * (len(args) -...]
    ppermute x16 -> x8, starting transfers between devices: 54 us -> 34.5 us  [the longest x6 28.6 us: shifted(): return lax.ppermute(value, axis, [(i, to(i)) for i in range(size)])]
    all_to_all x0 -> x1, blocking collectives: none -> 18.3 us  [spread(): return lax.all_to_all(value, 'seq', 0, 0, axis_index_groups=groups)]
  transfers between devices with their start and end apart: 17 -> 10, of which waited for: 8 -> 3; matrix products, arithmetic and copies ran while one was open for 9% -> 2% of each run, Pallas kernels for 0% -> 9%
where the time goes in v1:
time: 130 us; the launch traced here: 129 us
  starting transfers between devices  51.8 us (40%)
  waiting for transfers between devices  31.3 us (24%)
  Pallas kernels  19.7 us (15%)
  blocking collectives  18.3 us (14%)
  local copies, waits for them, and re-layouts  7.77 us (6%)
    ppermute x6, starting transfers between devices, shifted(): return lax.ppermute(value, axis, [(i, to(i)) for i in range(size)])  28.6 us
    ppermute x1, waiting for transfers between devices, local(): far = lax.ppermute(term, 'tp', [(t, t ^ 1) for t in range(2 * X)])  25.7 us
    pallas_call x8, Pallas kernels, call(): pl.pallas_call(kernel, in_specs=[smem] * scalars + [vmem] * (len(args) -...  19.7 us
    all_to_all x1, blocking collectives, spread(): return lax.all_to_all(value, 'seq', 0, 0, axis_index_groups=groups)  18.3 us
    all_to_all x2, starting transfers between devices, spread(): return lax.all_to_all(value, 'seq', 0, 0, axis_index_groups=groups)  17.3 us
    unnamed x19, local copies, waits for them, and re-layouts  7.77 us
    ppermute x6, waiting for transfers between devices, shifted(): return lax.ppermute(value, axis, [(i, to(i)) for i in range(size)])  5.61 us
    ppermute x1, starting transfers between devices, local(): other = lax.ppermute(own, 'seq', [(i, i ^ 1) for i in range(Z_HI * GROUP)])  3.8 us
  transfers between devices with their start and end apart: 10, of which 3 were waited for; matrix products, arithmetic and copies ran while one was open for 2% of the time, Pallas kernels for 9%

profile of v1, /device:TPU:1, one launch (start us, length us, event | category | flops | bytes accessed | tf_op | source)
XLA Modules:
  0.0 129.0 jit_solution(13267385485933131472)
XLA Ops:
  0.0 1.0 copy-done.2
  1.0 0.8 copy-done.5
  1.9 0.8 copy-done.7
  2.7 0.3 shard_map.91.own_ref._
  3.0 0.9 copy-done
  3.9 0.9 copy-done.3
  4.9 0.9 copy-done.4
  5.8 1.2 shard_map.95
  7.1 11.0 %all-to-all-start = ((bf16[16,320,128]{2,1,0:T(8,128)(2,1)}), bf16[16,320,128]{2,1,0:T(8,128)(2,1)}, u32[]{:S(2)}, u32[]{:S(2)}) async-start(bf16[16,320,128]{2,1,0:T(8,128)(2,1)} %shard_map.95), calls=%async_computation | async-start | bytes 2621440 | tf_op jit(solution)/shard_map/all_to_all | solution.py:27
  18.0 2.1 %collective-permute-start = (bf16[64,896]{1,0:T(8,128)(2,1)S(1)}, bf16[64,896]{1,0:T(8,128)(2,1)S(1)}, u32[]{:S(2)}, u32[]{:S(2)}) collective-permute-start(bf16[64,896]{1,0:T(8,128)(2,1)S(1)} %shard_map.91.own_ref._), channel_id=1, source_target_pairs={{0,64},{64,0},{128,192},{192,128},{256,320},{320,256},{384,448},{4... | collective-permute-start | bytes 344072 | tf_op jit(solution)/shard_map/ppermute | solution.py:199
  20.1 25.7 %collective-permute-done.far_ref = bf16[64,896]{1,0:T(8,128)(2,1)S(1)} collective-permute-done((bf16[64,896]{1,0:T(8,128)(2,1)S(1)}, bf16[64,896]{1,0:T(8,128)(2,1)S(1)}, u32[]{:S(2)}, u32[]{:S(2)}) %collective-permute-start) | collective-permute-done | bytes 114720 | tf_op jit(solution)/shard_map/ppermute | solution.py:199
  45.8 3.1 %collective-permute-start.1 = (bf16[64,1280]{1,0:T(8,128)(2,1)S(1)}, bf16[64,1280]{1,0:T(8,128)(2,1)S(1)}, u32[]{:S(2)}, u32[]{:S(2)}) collective-permute-start(bf16[64,1280]{1,0:T(8,128)(2,1)S(1)} %shard_map.92.n0), channel_id=1, source_target_pairs={{0,128},{64,192},{128,256},{192,320},{256,384},{320,448},{384,0},{... | collective-permute-start | bytes 491528 | tf_op jit(solution)/shard_map/ppermute | solution.py:33
  48.9 4.4 %collective-permute-start.2 = (bf16[64,1280]{1,0:T(8,128)(2,1)S(1)}, bf16[64,1280]{1,0:T(8,128)(2,1)S(1)}, u32[]{:S(2)}, u32[]{:S(2)}) collective-permute-start(bf16[64,1280]{1,0:T(8,128)(2,1)S(1)} %shard_map.92.n0), channel_id=1, source_target_pairs={{0,256},{64,320},{128,384},{192,448},{256,0},{320,64},{384,128},{4... | collective-permute-start | bytes 491528 | tf_op jit(solution)/shard_map/ppermute | solution.py:33
  53.3 3.1 %collective-permute-start.3 = (bf16[64,1280]{1,0:T(8,128)(2,1)S(1)}, bf16[64,1280]{1,0:T(8,128)(2,1)S(1)}, u32[]{:S(2)}, u32[]{:S(2)}) collective-permute-start(bf16[64,1280]{1,0:T(8,128)(2,1)S(1)} %shard_map.92.n0), channel_id=1, source_target_pairs={{0,384},{64,448},{128,0},{192,64},{256,128},{320,192},{384,256},{4... | collective-permute-start | bytes 491528 | tf_op jit(solution)/shard_map/ppermute | solution.py:33
  56.4 0.0 copy-start.6
  56.4 2.2 %copy.10 = bf16[320,8,2,256]{3,1,2,0:T(8,128)(2,1)S(1)} copy(bf16[320,8,2,256]{3,2,1,0:T(2,128)(2,1)} %bitcast.10) | data formatting | bytes 5242880
  58.6 0.1 pad_add_fusion.pos_ref
  58.7 0.0 collective-permute-done.2.n2
  58.7 0.9 collective-permute-done.3.n3
  59.6 1.2 shard_map.93
  60.8 5.8 %collective-permute-start.4 = (bf16[64,640]{1,0:T(8,128)(2,1)S(1)}, bf16[64,640]{1,0:T(8,128)(2,1)S(1)}, u32[]{:S(2)}, u32[]{:S(2)}) collective-permute-start(bf16[64,640]{1,0:T(8,128)(2,1)S(1)} %get-tuple-element.13), channel_id=1, source_target_pairs={{0,16},{1,17},{2,18},{3,19},{4,20},{5,21},{6,22},{7,23},{8,24},{9,... | collective-permute-start | bytes 245768 | tf_op jit(solution)/shard_map/ppermute | solution.py:33
  66.6 8.8 %collective-permute-start.5 = (bf16[64,640]{1,0:T(8,128)(2,1)S(1)}, bf16[64,640]{1,0:T(8,128)(2,1)S(1)}, u32[]{:S(2)}, u32[]{:S(2)}) collective-permute-start(bf16[64,640]{1,0:T(8,128)(2,1)S(1)} %get-tuple-element.14), channel_id=1, source_target_pairs={{0,32},{1,33},{2,34},{3,35},{4,36},{5,37},{6,38},{7,39},{8,40},{9,... | collective-permute-start | bytes 245768 | tf_op jit(solution)/shard_map/ppermute | solution.py:33
  75.5 3.4 %collective-permute-start.6 = (bf16[64,640]{1,0:T(8,128)(2,1)S(1)}, bf16[64,640]{1,0:T(8,128)(2,1)S(1)}, u32[]{:S(2)}, u32[]{:S(2)}) collective-permute-start(bf16[64,640]{1,0:T(8,128)(2,1)S(1)} %get-tuple-element.15), channel_id=1, source_target_pairs={{0,48},{1,49},{2,50},{3,51},{4,52},{5,53},{6,54},{7,55},{8,56},{9,... | collective-permute-start | bytes 245768 | tf_op jit(solution)/shard_map/ppermute | solution.py:33
  78.9 0.0 collective-permute-done.5.g2
  78.9 4.7 %collective-permute-done.6.g3 = bf16[64,640]{1,0:T(8,128)(2,1)S(1)} collective-permute-done((bf16[64,640]{1,0:T(8,128)(2,1)S(1)}, bf16[64,640]{1,0:T(8,128)(2,1)S(1)}, u32[]{:S(2)}, u32[]{:S(2)}) %collective-permute-start.6) | collective-permute-done | bytes 81952 | tf_op jit(solution)/shard_map/ppermute | solution.py:33
  83.6 1.0 shard_map.94
  84.5 3.8 %collective-permute-start.7 = (bf16[16,320,128]{2,1,0:T(8,128)(2,1)}, bf16[16,320,128]{2,1,0:T(8,128)(2,1)S(1)}, u32[]{:S(2)}, u32[]{:S(2)}) collective-permute-start(bf16[16,320,128]{2,1,0:T(8,128)(2,1)} %all-to-all-done.own_ref), channel_id=1, source_target_pairs={{0,1},{1,0},{2,3},{3,2},{4,5},{5,4},{6,7},{7,6},{8,9},{9,8},{10,11... | collective-permute-start | bytes 3932168 | tf_op jit(solution)/shard_map/ppermute | solution.py:217
  88.3 6.3 %all-to-all-start.1 = ((bf16[16,8,512]{2,1,0:T(8,128)(2,1)}), bf16[16,8,512]{2,1,0:T(8,128)(2,1)S(1)}, u32[]{:S(2)}, u32[]{:S(2)}) async-start(bf16[16,8,512]{2,1,0:T(8,128)(2,1)} %shard_map.94), calls=%async_computation.1 | async-start | bytes 262144 | tf_op jit(solution)/shard_map/all_to_all | solution.py:27
  94.7 0.0 collective-permute-done.7.other_ref
  94.7 9.3 %shard_map.96.o_ref = bf16[16,72,128]{2,1,0:T(8,128)(2,1)S(1)} custom-call(bf16[16,320,128]{2,1,0:T(8,128)(2,1)} %all-to-all-done.own_ref, bf16[16,320,128]{2,1,0:T(8,128)(2,1)S(1)} %collective-permute-done.7.other_ref), custom_call_target="tpu_custom_call" | custom-call | tf_op jit(solution)/shard_map/pallas_call | solution.py:49
  104.0 18.3 %all_to_all.15.back_ref = bf16[16,104,128]{2,1,0:T(8,128)(2,1)S(1)} all-to-all(bf16[16,104,128]{2,1,0:T(8,128)(2,1)S(1)} %shard_map.97), channel_id=1, replica_groups={{0,1,2,3,4,5,6,7,8,9,10,11,12,13,14,15},{16,17,18,19,20,21,22,23,24,25,..., dimensions={0} | all-to-all | bytes 851968 | tf_op jit(solution)/shard_map/all_to_all | solution.py:27
  122.3 6.7 %shard_map.98 = bf16[2,256,256]{2,1,0:T(8,128)(2,1)} custom-call(s32[1]{0:T(128)} %bitcast.pair_ref, s32[4]{0:T(128)S(1)} %copy-done.8, bf16[2,256,256]{2,1,0:T(8,128)(2,1)S(1)} %copy-done.1, bf16[16,104,128]{2,1,0:T(8,128)(2,1)S(1)} %all_to_all.15.back_ref), custom_call_target="tpu_custom_call" | custom-call | tf_op jit(solution)/shard_map/pallas_call | solution.py:49
  (17 shorter events, 0.1 us)
Async XLA Ops:
  0.0 1.0 copy-start.2
  1.0 0.8 copy-start.5
  1.9 0.8 copy-start.7
  3.0 1.0 copy-start
  3.9 0.9 copy-start.3
  4.9 0.9 copy-start.4
  7.1 77.5 %all-to-all-start = ((bf16[16,320,128]{2,1,0:T(8,128)(2,1)}), bf16[16,320,128]{2,1,0:T(8,128)(2,1)}, u32[]{:S(2)}, u32[]{:S(2)}) async-start(bf16[16,320,128]{2,1,0:T(8,128)(2,1)} %shard_map.95), calls=%async_computation | async-start | bytes 2621440 | tf_op jit(solution)/shard_map/all_to_all | solution.py:27
  18.0 27.8 %collective-permute-start = (bf16[64,896]{1,0:T(8,128)(2,1)S(1)}, bf16[64,896]{1,0:T(8,128)(2,1)S(1)}, u32[]{:S(2)}, u32[]{:S(2)}) collective-permute-start(bf16[64,896]{1,0:T(8,128)(2,1)S(1)} %shard_map.91.own_ref._), channel_id=1, source_target_pairs={{0,64},{64,0},{128,192},{192,128},{256,320},{320,256},{384,448},{4... | collective-permute-start | bytes 344072 | tf_op jit(solution)/shard_map/ppermute | solution.py:199
  45.8 12.9 %collective-permute-start.1 = (bf16[64,1280]{1,0:T(8,128)(2,1)S(1)}, bf16[64,1280]{1,0:T(8,128)(2,1)S(1)}, u32[]{:S(2)}, u32[]{:S(2)}) collective-permute-start(bf16[64,1280]{1,0:T(8,128)(2,1)S(1)} %shard_map.92.n0), channel_id=1, source_target_pairs={{0,128},{64,192},{128,256},{192,320},{256,384},{320,448},{384,0},{... | collective-permute-start | bytes 491528 | tf_op jit(solution)/shard_map/ppermute | solution.py:33
  48.9 9.8 %collective-permute-start.2 = (bf16[64,1280]{1,0:T(8,128)(2,1)S(1)}, bf16[64,1280]{1,0:T(8,128)(2,1)S(1)}, u32[]{:S(2)}, u32[]{:S(2)}) collective-permute-start(bf16[64,1280]{1,0:T(8,128)(2,1)S(1)} %shard_map.92.n0), channel_id=1, source_target_pairs={{0,256},{64,320},{128,384},{192,448},{256,0},{320,64},{384,128},{4... | collective-permute-start | bytes 491528 | tf_op jit(solution)/shard_map/ppermute | solution.py:33
  53.3 6.3 %collective-permute-start.3 = (bf16[64,1280]{1,0:T(8,128)(2,1)S(1)}, bf16[64,1280]{1,0:T(8,128)(2,1)S(1)}, u32[]{:S(2)}, u32[]{:S(2)}) collective-permute-start(bf16[64,1280]{1,0:T(8,128)(2,1)S(1)} %shard_map.92.n0), channel_id=1, source_target_pairs={{0,384},{64,448},{128,0},{192,64},{256,128},{320,192},{384,256},{4... | collective-permute-start | bytes 491528 | tf_op jit(solution)/shard_map/ppermute | solution.py:33
  56.4 3.3 %copy-start.6 = (bf16[512,64]{0,1:T(8,128)(2,1)S(1)}, bf16[512,64]{0,1:T(8,128)(2,1)}, u32[]{:S(2)}) copy-start(bf16[512,64]{0,1:T(8,128)(2,1)} %param.10) | copy-start | bytes 196612
  60.8 18.1 %collective-permute-start.4 = (bf16[64,640]{1,0:T(8,128)(2,1)S(1)}, bf16[64,640]{1,0:T(8,128)(2,1)S(1)}, u32[]{:S(2)}, u32[]{:S(2)}) collective-permute-start(bf16[64,640]{1,0:T(8,128)(2,1)S(1)} %get-tuple-element.13), channel_id=1, source_target_pairs={{0,16},{1,17},{2,18},{3,19},{4,20},{5,21},{6,22},{7,23},{8,24},{9,... | collective-permute-start | bytes 245768 | tf_op jit(solution)/shard_map/ppermute | solution.py:33
  66.6 12.3 %collective-permute-start.5 = (bf16[64,640]{1,0:T(8,128)(2,1)S(1)}, bf16[64,640]{1,0:T(8,128)(2,1)S(1)}, u32[]{:S(2)}, u32[]{:S(2)}) collective-permute-start(bf16[64,640]{1,0:T(8,128)(2,1)S(1)} %get-tuple-element.14), channel_id=1, source_target_pairs={{0,32},{1,33},{2,34},{3,35},{4,36},{5,37},{6,38},{7,39},{8,40},{9,... | collective-permute-start | bytes 245768 | tf_op jit(solution)/shard_map/ppermute | solution.py:33
  75.5 8.1 %collective-permute-start.6 = (bf16[64,640]{1,0:T(8,128)(2,1)S(1)}, bf16[64,640]{1,0:T(8,128)(2,1)S(1)}, u32[]{:S(2)}, u32[]{:S(2)}) collective-permute-start(bf16[64,640]{1,0:T(8,128)(2,1)S(1)} %get-tuple-element.15), channel_id=1, source_target_pairs={{0,48},{1,49},{2,50},{3,51},{4,52},{5,53},{6,54},{7,55},{8,56},{9,... | collective-permute-start | bytes 245768 | tf_op jit(solution)/shard_map/ppermute | solution.py:33
  84.5 10.1 %collective-permute-start.7 = (bf16[16,320,128]{2,1,0:T(8,128)(2,1)}, bf16[16,320,128]{2,1,0:T(8,128)(2,1)S(1)}, u32[]{:S(2)}, u32[]{:S(2)}) collective-permute-start(bf16[16,320,128]{2,1,0:T(8,128)(2,1)} %all-to-all-done.own_ref), channel_id=1, source_target_pairs={{0,1},{1,0},{2,3},{3,2},{4,5},{5,4},{6,7},{7,6},{8,9},{9,8},{10,11... | collective-permute-start | bytes 3932168 | tf_op jit(solution)/shard_map/ppermute | solution.py:217
  88.3 15.6 %all-to-all-start.1 = ((bf16[16,8,512]{2,1,0:T(8,128)(2,1)}), bf16[16,8,512]{2,1,0:T(8,128)(2,1)S(1)}, u32[]{:S(2)}, u32[]{:S(2)}) async-start(bf16[16,8,512]{2,1,0:T(8,128)(2,1)} %shard_map.94), calls=%async_computation.1 | async-start | bytes 262144 | tf_op jit(solution)/shard_map/all_to_all | solution.py:27
  103.9 18.4 %copy-start.1 = (bf16[2,256,256]{2,1,0:T(8,128)(2,1)S(1)}, bf16[2,256,256]{2,1,0:T(8,128)(2,1)}, u32[]{:S(2)}) copy-start(bf16[2,256,256]{2,1,0:T(8,128)(2,1)} %q_ref.3) | copy-start | bytes 786436
  103.9 18.4 %copy-start.8 = (s32[4]{0:T(128)S(1)}, s32[4]{0:T(128)}, u32[]{:S(2)}) copy-start(s32[4]{0:T(128)} %live_ref.1) | copy-start | bytes 52

commit v2 on v1

v2 whole, which is shorter than its diff:
```python
import math

import jax
import jax.numpy as jnp
from jax import lax
from jax.experimental import pallas as pl
from jax.experimental.pallas import tpu as pltpu
from jax.sharding import PartitionSpec as P


TXT = 128
HD = 128
NEG = -1e30
BF = jnp.bfloat16
F32 = jnp.float32
SCALE = 1.0 / math.sqrt(HD)
LOG2E = math.log2(math.e)

X, Z_HI, GROUP = 4, 4, 16
NT = (((1,), (1,)), ((), ()))
TN = (((0,), (0,)), ((), ()))


def spread(value):
    groups = [[p * GROUP + m for m in range(GROUP)] for p in range(Z_HI)]
    return lax.all_to_all(value, "seq", 0, 0, axis_index_groups=groups)


def shifted(value, axis, span, stride, step):
    size = lax.axis_size(axis)
    to = lambda i: i + ((i // stride % span + step) % span - i // stride % span) * stride
    return lax.ppermute(value, axis, [(i, to(i)) for i in range(size)])


KEYS, PIECE = TXT, 64
SENT = 2 * KEYS + PIECE
LSE, TEXT = PIECE, PIECE + 8
BACK = TEXT + 32


def duty(m):
    return m // 8, m // 2 % 2, m % 2, m // 4 % 2 * 2 + m % 2


def call(kernel, args, outs, scalars=0, mib=4, hbm=0, hbm_outs=0, **extra):
    vmem = pl.BlockSpec(memory_space=pltpu.VMEM)
    smem = pl.BlockSpec(memory_space=pltpu.SMEM)
    far = pl.BlockSpec(memory_space=pltpu.HBM)
    result = pl.pallas_call(
        kernel,
        in_specs=[smem] * scalars + [far] * hbm + [vmem] * (len(args) - scalars - hbm),
        out_specs=[far] * hbm_outs + [vmem] * (len(outs) - hbm_outs),
        out_shape=outs,
        compiler_params=pltpu.CompilerParams(vmem_limit_bytes=mib << 20),
        **extra,
    )(*args)
    return result[0] if len(outs) == 1 else result


def after(value, *others):
    return lax.optimization_barrier((value, *others))[0]


def shape(*dims, dtype=BF):
    return jax.ShapeDtypeStruct(dims, dtype)


def start_kernel(k_hbm, v_hbm, q_hbm, ctx_hbm, w_hbm, cap_hbm, image_hbm, out_ref, k_ref, v_ref, q_ref, ctx_ref, w_ref, cap_ref, image_ref, sems):
    loads = [
        pltpu.make_async_copy(source, target, sems.at[i])
        for i, (source, target) in enumerate(
            ((k_hbm, k_ref), (v_hbm, v_ref), (q_hbm, q_ref), (ctx_hbm, ctx_ref), (w_hbm, w_ref), (cap_hbm, cap_ref))
        )
    ]
    for load in loads:
        load.start()
    for load in loads[:3]:
        load.wait()
    moves = []
    for m in range(GROUP):
        side, head, keys, piece = duty(m)
        cols = slice(head * HD, (head + 1) * HD)
        rows = slice(keys * KEYS, (keys + 1) * KEYS)
        image_ref[m, :KEYS] = k_ref[side, rows, cols]
        image_ref[m, KEYS : 2 * KEYS] = v_ref[side, rows, cols]
        image_ref[m, 2 * KEYS :] = q_ref[side, piece * PIECE : (piece + 1) * PIECE, cols]
        moves.append(pltpu.make_async_copy(image_ref.at[m], image_hbm.at[m], sems.at[len(loads) + m]))
        moves[-1].start()
    for load in loads[3:]:
        load.wait()
    term = lax.dot_general(w_ref[...], ctx_ref[...], NT, preferred_element_type=F32)
    rows = term.shape[1]
    out_ref[:, :rows] = term.astype(BF)
    out_ref[:, rows:] = cap_ref[...]
    for move in moves:
        move.wait()


def near_kernel(own_ref, far_ref, out_ref):
    cols = (out_ref.shape[1] - own_ref.shape[1])
    rows = own_ref.shape[1] - cols
    out_ref[:, :rows] = (own_ref[:, :rows].astype(F32) + far_ref[:, :rows].astype(F32)).astype(BF)
    out_ref[:, rows:] = jnp.concatenate([own_ref[:, rows:], far_ref[:, rows:]], axis=1)


def joint_kernel(pos_ref, n0, n1, n2, n3, res_ref, w_ref, o0, o1, o2, o3, hid_ref):
    x, yhi, zhi = pos_ref[0], pos_ref[1], pos_ref[2]
    rows = hid_ref.shape[1]
    cols = w_ref.shape[0] // (2 * X)
    total = res_ref[...].astype(F32)
    joint = jnp.zeros((total.shape[0], w_ref.shape[1]), F32)
    for step, ref in enumerate((n0, n1, n2, n3)):
        total = total + ref[:, :rows].astype(F32)
        source = (x + X - step) % X
        for far in range(2):
            block = source * 2 + (yhi + far) % 2
            first = pl.multiple_of(block * cols, cols)
            cap = ref[:, rows + far * cols : rows + (far + 1) * cols]
            joint += jnp.dot(cap, w_ref[pl.ds(first, cols), :], preferred_element_type=F32)
    hid_ref[...] = total.astype(BF)
    joint = joint.astype(BF)
    for step, ref in enumerate((o0, o1, o2, o3)):
        first = pl.multiple_of((zhi + step) % Z_HI * TXT, TXT)
        ref[:, :TXT] = hid_ref[:, pl.ds(first, TXT)]
        ref[:, TXT:] = joint


def part_kernel(g0, g1, g2, g3, out_ref):
    part = None
    for ref in (g0, g1, g2, g3):
        term = lax.dot_general(ref[:, :TXT], ref[:, TXT:], TN, preferred_element_type=F32)
        part = term if part is None else part + term
    out_ref[...] = part.astype(BF).reshape(out_ref.shape)


def sum_kernel(part_ref, o_ref, out_ref):
    total = jnp.sum(part_ref[...].astype(F32), axis=0)
    text = jnp.concatenate([total[:, i * HD : (i + 1) * HD] for i in range(4)], axis=0).astype(BF)
    for m in range(GROUP):
        out_ref[m, :TEXT] = o_ref[m]
        out_ref[m, TEXT:] = text


BLOCK = 512


def image_kernel(own_ref, other_ref, out_ref):
    scale = SCALE * LOG2E
    count = BLOCK // PIECE
    for block in range(GROUP // count):
        members = slice(block * count, (block + 1) * count)
        q = own_ref[members, 2 * KEYS :].reshape(BLOCK, HD)
        top, total, acc = jnp.full((BLOCK, 1), NEG, F32), 0.0, 0.0
        for ref in (own_ref, other_ref):
            s = lax.dot_general(q, ref[:, :KEYS].reshape(-1, HD), NT, preferred_element_type=F32)
            old, top = top, jnp.maximum(top, jnp.max(s, axis=1, keepdims=True))
            p = jnp.exp2(s * scale - top * scale)
            factor = jnp.exp2(old * scale - top * scale)
            values = ref[:, KEYS : 2 * KEYS].reshape(-1, HD)
            total = total * factor + jnp.sum(p, axis=1, keepdims=True)
            acc = acc * factor + jnp.dot(p.astype(BF), values, preferred_element_type=F32)
        out_ref[members, :PIECE] = (acc / total).astype(BF).reshape(count, PIECE, HD)
        rest = top * SCALE + jnp.log(total)
        rest = jnp.transpose(jnp.broadcast_to(rest, (BLOCK, HD)))[:8]
        first = rest.astype(BF).astype(F32)
        rest = rest - first
        second = rest.astype(BF).astype(F32)
        place = lax.broadcasted_iota(jnp.int32, rest.shape, 0)
        lse = jnp.where(place == 0, first, jnp.where(place == 1, second, rest - second))
        for i in range(count):
            row = jnp.concatenate([lse[:, i * PIECE : (i + 1) * PIECE]] * 2, axis=1)
            out_ref[block * count + i, LSE:TEXT] = row.astype(BF)


def text_kernel(pair_ref, live_ref, q_ref, back_ref, out_ref):
    live = live_ref[pair_ref[0]]
    text = [
        back_ref[:, TEXT + 8 * i : TEXT + 8 * i + 8].astype(F32).reshape(TXT, HD).astype(BF) for i in range(4)
    ]
    rows = q_ref.shape[1]
    kept = lax.broadcasted_iota(jnp.int32, (rows, TXT), 1) < live
    low = lax.broadcasted_iota(jnp.int32, (8, HD), 1) < PIECE
    for side in range(2):
        for head in range(2):
            owners = sorted((m for m in range(GROUP) if duty(m)[:2] == (side, head)), key=lambda m: duty(m)[3])
            cols = slice(head * HD, (head + 1) * HD)
            s = lax.dot_general(q_ref[side, :, cols], text[head], NT, preferred_element_type=F32) * SCALE
            s = jnp.where(kept, s, NEG)
            lse = []
            for m in owners:
                tail = back_ref[m, LSE:TEXT].astype(F32)
                lse.append(jnp.broadcast_to(tail[:1] + tail[1:2] + tail[2:3], tail.shape))
            lse = jnp.concatenate([jnp.where(low, lse[0], lse[1]), jnp.where(low, lse[2], lse[3])], axis=1)
            lse = jnp.transpose(lse)[:, :1]
            top = jnp.maximum(jnp.max(s, axis=1, keepdims=True), lse)
            p = jnp.exp(s - top)
            image = jnp.exp(lse - top)
            total = image + jnp.sum(p, axis=1, keepdims=True)
            acc = jnp.dot(p.astype(BF), text[2 + head], preferred_element_type=F32)
            acc += image * jnp.concatenate([back_ref[m, :PIECE] for m in owners], axis=0).astype(F32)
            out_ref[side, :, cols] = (acc / total).astype(BF)


def local(
    llama_context,
    llama_residual,
    w_attn_out,
    w_caption,
    w_text_kv,
    prompt_length,
    image_query,
    image_key,
    image_value,
):
    tp, seq = lax.axis_index("tp"), lax.axis_index("seq")
    pos = jnp.stack((tp >> 1, tp & 1, seq >> 4))
    feats, text_rows = w_attn_out.shape[1], llama_context.shape[0]
    w_kv = w_text_kv.reshape(w_text_kv.shape[0], -1)
    kv_cols = w_kv.shape[1]

    cap_cols = w_caption.shape[1]
    image, term = call(
        start_kernel,
        (image_key, image_value, image_query, llama_context, w_attn_out.T, w_caption),
        [shape(GROUP, SENT, HD), shape(feats, text_rows + cap_cols)],
        mib=60,
        hbm=6,
        hbm_outs=1,
        scratch_shapes=[
            *[pltpu.VMEM(image_query.shape, BF)] * 3,
            pltpu.VMEM(llama_context.shape, BF),
            pltpu.VMEM(w_attn_out.shape[::-1], BF),
            pltpu.VMEM(w_caption.shape, BF),
            pltpu.VMEM((GROUP, SENT, HD), BF),
            pltpu.SemaphoreType.DMA((6 + GROUP,)),
        ],
    )
    far = lax.ppermute(term, "tp", [(t, t ^ 1) for t in range(2 * X)])
    own = spread(image)

    near = call(near_kernel, (term, far), [shape(feats, text_rows + 2 * cap_cols)])
    ring = [near] + [shifted(near, "tp", X, 2, step) for step in range(1, X)]
    sends = call(
        joint_kernel,
        (pos, *ring, llama_residual.T, w_kv),
        [shape(feats, TXT + kv_cols)] * Z_HI,
        scalars=1,
        mib=8,
        scratch_shapes=[pltpu.VMEM((feats, text_rows), BF)],
    )
    parts = [sends[0]] + [shifted(sends[step], "seq", Z_HI, GROUP, step) for step in range(1, Z_HI)]
    own = after(own, sends[0])
    other = lax.ppermute(own, "seq", [(i, i ^ 1) for i in range(Z_HI * GROUP)])
    part = call(part_kernel, parts, [shape(GROUP, TXT // GROUP, kv_cols)])
    part = spread(part)
    o = call(image_kernel, (own, other), [shape(GROUP, TEXT, HD)], mib=32)
    back = call(sum_kernel, (after(part, o), o), [shape(GROUP, BACK, HD)])
    back = spread(back)
    return call(text_kernel, (pos[2:], prompt_length, image_query, back), [shape(*image_query.shape)], scalars=2)


def solution(mesh):
    placed = (
        P(None, "tp"),
        P(None, "seq"),
        P("tp", "seq"),
        P("seq", "tp"),
        P(None, None, "tp"),
        P(),
        P(None, "seq", "tp"),
        P(None, "seq", "tp"),
        P(None, "seq", "tp"),
    )

    return jax.shard_map(local, mesh=mesh, in_specs=placed, out_specs=P(None, "seq", "tp"), check_vma=False)
```

time: 130 us -> 122 us (0.938)
  local copies, waits for them, and re-layouts: 7.77 us -> 2.88 us
  Pallas kernels: 19.7 us -> 15.3 us
  waiting for transfers between devices: 31.3 us -> 34.9 us
  starting transfers between devices: 51.8 us -> 49.7 us
    unnamed x19 -> x11, local copies, waits for them, and re-layouts: 7.77 us -> 2.88 us
    pallas_call x8 -> x7, Pallas kernels: 19.7 us -> 15.3 us  [call(): pl.pallas_call(kernel, in_specs=[smem] * scalars + [far] * hbm + [vmem] *...]
    ppermute x6, waiting for transfers between devices: 5.61 us -> 9.24 us  [shifted(): return lax.ppermute(value, axis, [(i, to(i)) for i in range(size)])]
  transfers between devices with their start and end apart: 10 -> 10, of which waited for: 3 -> 5; matrix products, arithmetic and copies ran while one was open for 2% -> 2% of each run, Pallas kernels for 9% -> 8%
where the time goes in v2:
time: 122 us; the launch traced here: 121 us
  starting transfers between devices  49.7 us (41%)
  waiting for transfers between devices  34.9 us (29%)
  blocking collectives  18.3 us (15%)
  Pallas kernels  15.3 us (13%)
  local copies, waits for them, and re-layouts  2.88 us (2%)
    ppermute x6, starting transfers between devices, shifted(): return lax.ppermute(value, axis, [(i, to(i)) for i in range(size)])  27.3 us
    ppermute x1, waiting for transfers between devices, local(): far = lax.ppermute(term, 'tp', [(t, t ^ 1) for t in range(2 * X)])  25.6 us
    all_to_all x1, blocking collectives, spread(): return lax.all_to_all(value, 'seq', 0, 0, axis_index_groups=groups)  18.3 us
    all_to_all x2, starting transfers between devices, spread(): return lax.all_to_all(value, 'seq', 0, 0, axis_index_groups=groups)  17 us
    pallas_call x7, Pallas kernels, call(): pl.pallas_call(kernel, in_specs=[smem] * scalars + [far] * hbm + [vmem] *...  15.3 us
    ppermute x6, waiting for transfers between devices, shifted(): return lax.ppermute(value, axis, [(i, to(i)) for i in range(size)])  9.24 us
    ppermute x1, starting transfers between devices, local(): other = lax.ppermute(own, 'seq', [(i, i ^ 1) for i in range(Z_HI * GROUP)])  3.18 us
    unnamed x11, local copies, waits for them, and re-layouts  2.88 us
  transfers between devices with their start and end apart: 10, of which 5 were waited for; matrix products, arithmetic and copies ran while one was open for 2% of the time, Pallas kernels for 8%

profile of v2, /device:TPU:1, one launch (start us, length us, event | category | flops | bytes accessed | tf_op | source)
XLA Modules:
  0.0 121.3 jit_solution(10309437918107171337)
XLA Ops:
  0.0 3.0 %shard_map.91 = (bf16[16,320,128]{2,1,0:T(8,128)(2,1)}, bf16[64,832]{1,0:T(8,128)(2,1)}) custom-call(bf16[2,256,256]{2,1,0:T(8,128)(2,1)} %k_hbm.1, bf16[2,256,256]{2,1,0:T(8,128)(2,1)} %v_hbm.1, bf16[2,256,256]{2,1,0:T(8,128)(2,1)} %q_ref.1, bf16[512,512]{1,0:T(8,128)(2,1)} %ctx_hbm.1, bf16[64,512]{1,0:T(8,128)(2,1)} %bitcast.10, bf16[64,320]{1,0:T(8,128)(2,1)} %cap_hbm.1), custom_call_target="tpu_custom_call" | custom-call | tf_op jit(solution)/shard_map/pallas_call | solution.py:49
  3.0 0.0 copy-start.1
  3.1 11.1 %all-to-all-start.1 = ((bf16[16,320,128]{2,1,0:T(8,128)(2,1)}), bf16[16,320,128]{2,1,0:T(8,128)(2,1)}, u32[]{:S(2)}, u32[]{:S(2)}) async-start(bf16[16,320,128]{2,1,0:T(8,128)(2,1)} %get-tuple-element.18), calls=%async_computation.1 | async-start | bytes 2621440 | tf_op jit(solution)/shard_map/all_to_all | solution.py:26
  14.2 2.1 %collective-permute-start = (bf16[64,832]{1,0:T(8,128)(2,1)S(1)}, bf16[64,832]{1,0:T(8,128)(2,1)S(1)}, u32[]{:S(2)}, u32[]{:S(2)}) collective-permute-start(bf16[64,832]{1,0:T(8,128)(2,1)S(1)} %copy-done.1), channel_id=1, source_target_pairs={{0,64},{64,0},{128,192},{192,128},{256,320},{320,256},{384,448},{4... | collective-permute-start | bytes 319496 | tf_op jit(solution)/shard_map/ppermute | solution.py:238
  16.3 25.6 %collective-permute-done.far_ref = bf16[64,832]{1,0:T(8,128)(2,1)S(1)} collective-permute-done((bf16[64,832]{1,0:T(8,128)(2,1)S(1)}, bf16[64,832]{1,0:T(8,128)(2,1)S(1)}, u32[]{:S(2)}, u32[]{:S(2)}) %collective-permute-start) | collective-permute-done | bytes 106528 | tf_op jit(solution)/shard_map/ppermute | solution.py:238
  41.9 0.1 shard_map.92.n0
  42.0 4.4 %collective-permute-start.3 = (bf16[64,1152]{1,0:T(8,128)(2,1)S(1)}, bf16[64,1152]{1,0:T(8,128)(2,1)S(1)}, u32[]{:S(2)}, u32[]{:S(2)}) collective-permute-start(bf16[64,1152]{1,0:T(8,128)(2,1)S(1)} %shard_map.92.n0), channel_id=1, source_target_pairs={{0,384},{64,448},{128,0},{192,64},{256,128},{320,192},{384,256},{4... | collective-permute-start | bytes 442376 | tf_op jit(solution)/shard_map/ppermute | solution.py:32
  46.4 2.4 %collective-permute-start.2 = (bf16[64,1152]{1,0:T(8,128)(2,1)S(1)}, bf16[64,1152]{1,0:T(8,128)(2,1)S(1)}, u32[]{:S(2)}, u32[]{:S(2)}) collective-permute-start(bf16[64,1152]{1,0:T(8,128)(2,1)S(1)} %shard_map.92.n0), channel_id=1, source_target_pairs={{0,256},{64,320},{128,384},{192,448},{256,0},{320,64},{384,128},{4... | collective-permute-start | bytes 442376 | tf_op jit(solution)/shard_map/ppermute | solution.py:32
  48.8 2.5 %collective-permute-start.1 = (bf16[64,1152]{1,0:T(8,128)(2,1)S(1)}, bf16[64,1152]{1,0:T(8,128)(2,1)S(1)}, u32[]{:S(2)}, u32[]{:S(2)}) collective-permute-start(bf16[64,1152]{1,0:T(8,128)(2,1)S(1)} %shard_map.92.n0), channel_id=1, source_target_pairs={{0,128},{64,192},{128,256},{192,320},{256,384},{320,448},{384,0},{... | collective-permute-start | bytes 442376 | tf_op jit(solution)/shard_map/ppermute | solution.py:32
  51.4 0.0 copy-start.2
  51.4 2.2 %copy.10 = bf16[320,8,2,256]{3,1,2,0:T(8,128)(2,1)S(1)} copy(bf16[320,8,2,256]{3,2,1,0:T(2,128)(2,1)} %bitcast.9) | data formatting | bytes 5242880
  53.6 0.1 pad_add_fusion.pos_ref
  53.7 0.0 collective-permute-done.3.n3
  53.7 0.5 collective-permute-done.2.n2
  54.2 3.9 %collective-permute-done.1.n1 = bf16[64,1152]{1,0:T(8,128)(2,1)S(1)} collective-permute-done((bf16[64,1152]{1,0:T(8,128)(2,1)S(1)}, bf16[64,1152]{1,0:T(8,128)(2,1)S(1)}, u32[]{:S(2)}, u32[]{:S(2)}) %collective-permute-start.1) | collective-permute-done | bytes 147488 | tf_op jit(solution)/shard_map/ppermute | solution.py:32
  58.0 1.2 shard_map.93
  59.3 0.0 copy-start.4
  59.3 0.6 copy-done.4
  59.9 0.0 all-to-all-done.1.own_ref
  59.9 3.2 %collective-permute-start.7 = (bf16[16,320,128]{2,1,0:T(8,128)(2,1)}, bf16[16,320,128]{2,1,0:T(8,128)(2,1)S(1)}, u32[]{:S(2)}, u32[]{:S(2)}) collective-permute-start(bf16[16,320,128]{2,1,0:T(8,128)(2,1)} %all-to-all-done.1.own_ref), channel_id=1, source_target_pairs={{0,1},{1,0},{2,3},{3,2},{4,5},{5,4},{6,7},{7,6},{8,9},{9,8},{10,11... | collective-permute-start | bytes 3932168 | tf_op jit(solution)/shard_map/ppermute | solution.py:253
  63.1 5.8 %collective-permute-start.4 = (bf16[64,640]{1,0:T(8,128)(2,1)}, bf16[64,640]{1,0:T(8,128)(2,1)S(1)}, u32[]{:S(2)}, u32[]{:S(2)}) collective-permute-start(bf16[64,640]{1,0:T(8,128)(2,1)} %copy-done.4), channel_id=1, source_target_pairs={{0,16},{1,17},{2,18},{3,19},{4,20},{5,21},{6,22},{7,23},{8,24},{9,... | collective-permute-start | bytes 245768 | tf_op jit(solution)/shard_map/ppermute | solution.py:32
  68.9 8.8 %collective-permute-start.5 = (bf16[64,640]{1,0:T(8,128)(2,1)S(1)}, bf16[64,640]{1,0:T(8,128)(2,1)S(1)}, u32[]{:S(2)}, u32[]{:S(2)}) collective-permute-start(bf16[64,640]{1,0:T(8,128)(2,1)S(1)} %get-tuple-element.16), channel_id=1, source_target_pairs={{0,32},{1,33},{2,34},{3,35},{4,36},{5,37},{6,38},{7,39},{8,40},{9,... | collective-permute-start | bytes 245768 | tf_op jit(solution)/shard_map/ppermute | solution.py:32
  77.7 3.4 %collective-permute-start.6 = (bf16[64,640]{1,0:T(8,128)(2,1)S(1)}, bf16[64,640]{1,0:T(8,128)(2,1)S(1)}, u32[]{:S(2)}, u32[]{:S(2)}) collective-permute-start(bf16[64,640]{1,0:T(8,128)(2,1)S(1)} %get-tuple-element.17), channel_id=1, source_target_pairs={{0,48},{1,49},{2,50},{3,51},{4,52},{5,53},{6,54},{7,55},{8,56},{9,... | collective-permute-start | bytes 245768 | tf_op jit(solution)/shard_map/ppermute | solution.py:32
  81.1 0.0 collective-permute-done.4.g1
  81.1 2.7 %collective-permute-done.5.g2 = bf16[64,640]{1,0:T(8,128)(2,1)S(1)} collective-permute-done((bf16[64,640]{1,0:T(8,128)(2,1)S(1)}, bf16[64,640]{1,0:T(8,128)(2,1)S(1)}, u32[]{:S(2)}, u32[]{:S(2)}) %collective-permute-start.5) | collective-permute-done | bytes 81952 | tf_op jit(solution)/shard_map/ppermute | solution.py:32
  83.9 2.2 %collective-permute-done.6.g3 = bf16[64,640]{1,0:T(8,128)(2,1)S(1)} collective-permute-done((bf16[64,640]{1,0:T(8,128)(2,1)S(1)}, bf16[64,640]{1,0:T(8,128)(2,1)S(1)}, u32[]{:S(2)}, u32[]{:S(2)}) %collective-permute-start.6) | collective-permute-done | bytes 81952 | tf_op jit(solution)/shard_map/ppermute | solution.py:32
  86.0 1.0 shard_map.94
  87.0 5.9 %all-to-all-start = ((bf16[16,8,512]{2,1,0:T(8,128)(2,1)}), bf16[16,8,512]{2,1,0:T(8,128)(2,1)S(1)}, u32[]{:S(2)}, u32[]{:S(2)}) async-start(bf16[16,8,512]{2,1,0:T(8,128)(2,1)} %shard_map.94), calls=%async_computation | async-start | bytes 262144 | tf_op jit(solution)/shard_map/all_to_all | solution.py:26
  92.9 7.3 %shard_map.95.o_ref = bf16[16,72,128]{2,1,0:T(8,128)(2,1)S(1)} custom-call(bf16[16,320,128]{2,1,0:T(8,128)(2,1)} %all-to-all-done.1.own_ref, bf16[16,320,128]{2,1,0:T(8,128)(2,1)S(1)} %collective-permute-done.7.other_ref), custom_call_target="tpu_custom_call" | custom-call | tf_op jit(solution)/shard_map/pallas_call | solution.py:49
  100.2 0.0 all-to-all-done.part_ref
  100.3 18.3 %all_to_all.15.back_ref = bf16[16,104,128]{2,1,0:T(8,128)(2,1)S(1)} all-to-all(bf16[16,104,128]{2,1,0:T(8,128)(2,1)S(1)} %shard_map.96), channel_id=1, replica_groups={{0,1,2,3,4,5,6,7,8,9,10,11,12,13,14,15},{16,17,18,19,20,21,22,23,24,25,..., dimensions={0} | all-to-all | bytes 851968 | tf_op jit(solution)/shard_map/all_to_all | solution.py:26
  118.6 2.7 %shard_map.97 = bf16[2,256,256]{2,1,0:T(8,128)(2,1)} custom-call(s32[1]{0:T(128)} %bitcast.pair_ref, s32[4]{0:T(128)S(1)} %copy-done.3, bf16[2,256,256]{2,1,0:T(8,128)(2,1)S(1)} %copy-done, bf16[16,104,128]{2,1,0:T(8,128)(2,1)S(1)} %all_to_all.15.back_ref), custom_call_target="tpu_custom_call" | custom-call | tf_op jit(solution)/shard_map/pallas_call | solution.py:49
  (8 shorter events, 0.1 us)
Async XLA Ops:
  3.0 11.1 %copy-start.1 = (bf16[64,832]{1,0:T(8,128)(2,1)S(1)}, bf16[64,832]{1,0:T(8,128)(2,1)}, u32[]{:S(2)}) copy-start(bf16[64,832]{1,0:T(8,128)(2,1)} %get-tuple-element.13.own_ref) | copy-start | bytes 319492
  3.1 56.8 %all-to-all-start.1 = ((bf16[16,320,128]{2,1,0:T(8,128)(2,1)}), bf16[16,320,128]{2,1,0:T(8,128)(2,1)}, u32[]{:S(2)}, u32[]{:S(2)}) async-start(bf16[16,320,128]{2,1,0:T(8,128)(2,1)} %get-tuple-element.18), calls=%async_computation.1 | async-start | bytes 2621440 | tf_op jit(solution)/shard_map/all_to_all | solution.py:26
  14.2 27.8 %collective-permute-start = (bf16[64,832]{1,0:T(8,128)(2,1)S(1)}, bf16[64,832]{1,0:T(8,128)(2,1)S(1)}, u32[]{:S(2)}, u32[]{:S(2)}) collective-permute-start(bf16[64,832]{1,0:T(8,128)(2,1)S(1)} %copy-done.1), channel_id=1, source_target_pairs={{0,64},{64,0},{128,192},{192,128},{256,320},{320,256},{384,448},{4... | collective-permute-start | bytes 319496 | tf_op jit(solution)/shard_map/ppermute | solution.py:238
  42.0 11.7 %collective-permute-start.3 = (bf16[64,1152]{1,0:T(8,128)(2,1)S(1)}, bf16[64,1152]{1,0:T(8,128)(2,1)S(1)}, u32[]{:S(2)}, u32[]{:S(2)}) collective-permute-start(bf16[64,1152]{1,0:T(8,128)(2,1)S(1)} %shard_map.92.n0), channel_id=1, source_target_pairs={{0,384},{64,448},{128,0},{192,64},{256,128},{320,192},{384,256},{4... | collective-permute-start | bytes 442376 | tf_op jit(solution)/shard_map/ppermute | solution.py:32
  46.4 7.8 %collective-permute-start.2 = (bf16[64,1152]{1,0:T(8,128)(2,1)S(1)}, bf16[64,1152]{1,0:T(8,128)(2,1)S(1)}, u32[]{:S(2)}, u32[]{:S(2)}) collective-permute-start(bf16[64,1152]{1,0:T(8,128)(2,1)S(1)} %shard_map.92.n0), channel_id=1, source_target_pairs={{0,256},{64,320},{128,384},{192,448},{256,0},{320,64},{384,128},{4... | collective-permute-start | bytes 442376 | tf_op jit(solution)/shard_map/ppermute | solution.py:32
  48.8 9.2 %collective-permute-start.1 = (bf16[64,1152]{1,0:T(8,128)(2,1)S(1)}, bf16[64,1152]{1,0:T(8,128)(2,1)S(1)}, u32[]{:S(2)}, u32[]{:S(2)}) collective-permute-start(bf16[64,1152]{1,0:T(8,128)(2,1)S(1)} %shard_map.92.n0), channel_id=1, source_target_pairs={{0,128},{64,192},{128,256},{192,320},{256,384},{320,448},{384,0},{... | collective-permute-start | bytes 442376 | tf_op jit(solution)/shard_map/ppermute | solution.py:32
  51.4 6.7 %copy-start.2 = (bf16[512,64]{0,1:T(8,128)(2,1)S(1)}, bf16[512,64]{0,1:T(8,128)(2,1)}, u32[]{:S(2)}) copy-start(bf16[512,64]{0,1:T(8,128)(2,1)} %param.10) | copy-start | bytes 196612
  59.3 0.6 copy-start.4
  59.9 33.0 %collective-permute-start.7 = (bf16[16,320,128]{2,1,0:T(8,128)(2,1)}, bf16[16,320,128]{2,1,0:T(8,128)(2,1)S(1)}, u32[]{:S(2)}, u32[]{:S(2)}) collective-permute-start(bf16[16,320,128]{2,1,0:T(8,128)(2,1)} %all-to-all-done.1.own_ref), channel_id=1, source_target_pairs={{0,1},{1,0},{2,3},{3,2},{4,5},{5,4},{6,7},{7,6},{8,9},{9,8},{10,11... | collective-permute-start | bytes 3932168 | tf_op jit(solution)/shard_map/ppermute | solution.py:253
  63.1 18.1 %collective-permute-start.4 = (bf16[64,640]{1,0:T(8,128)(2,1)}, bf16[64,640]{1,0:T(8,128)(2,1)S(1)}, u32[]{:S(2)}, u32[]{:S(2)}) collective-permute-start(bf16[64,640]{1,0:T(8,128)(2,1)} %copy-done.4), channel_id=1, source_target_pairs={{0,16},{1,17},{2,18},{3,19},{4,20},{5,21},{6,22},{7,23},{8,24},{9,... | collective-permute-start | bytes 245768 | tf_op jit(solution)/shard_map/ppermute | solution.py:32
  68.9 15.0 %collective-permute-start.5 = (bf16[64,640]{1,0:T(8,128)(2,1)S(1)}, bf16[64,640]{1,0:T(8,128)(2,1)S(1)}, u32[]{:S(2)}, u32[]{:S(2)}) collective-permute-start(bf16[64,640]{1,0:T(8,128)(2,1)S(1)} %get-tuple-element.16), channel_id=1, source_target_pairs={{0,32},{1,33},{2,34},{3,35},{4,36},{5,37},{6,38},{7,39},{8,40},{9,... | collective-permute-start | bytes 245768 | tf_op jit(solution)/shard_map/ppermute | solution.py:32
  77.7 8.3 %collective-permute-start.6 = (bf16[64,640]{1,0:T(8,128)(2,1)S(1)}, bf16[64,640]{1,0:T(8,128)(2,1)S(1)}, u32[]{:S(2)}, u32[]{:S(2)}) collective-permute-start(bf16[64,640]{1,0:T(8,128)(2,1)S(1)} %get-tuple-element.17), channel_id=1, source_target_pairs={{0,48},{1,49},{2,50},{3,51},{4,52},{5,53},{6,54},{7,55},{8,56},{9,... | collective-permute-start | bytes 245768 | tf_op jit(solution)/shard_map/ppermute | solution.py:32
  87.0 13.2 %all-to-all-start = ((bf16[16,8,512]{2,1,0:T(8,128)(2,1)}), bf16[16,8,512]{2,1,0:T(8,128)(2,1)S(1)}, u32[]{:S(2)}, u32[]{:S(2)}) async-start(bf16[16,8,512]{2,1,0:T(8,128)(2,1)} %shard_map.94), calls=%async_computation | async-start | bytes 262144 | tf_op jit(solution)/shard_map/all_to_all | solution.py:26
  100.2 18.4 %copy-start = (bf16[2,256,256]{2,1,0:T(8,128)(2,1)S(1)}, bf16[2,256,256]{2,1,0:T(8,128)(2,1)}, u32[]{:S(2)}) copy-start(bf16[2,256,256]{2,1,0:T(8,128)(2,1)} %q_ref.1) | copy-start | bytes 786436
  100.2 18.4 %copy-start.3 = (s32[4]{0:T(128)S(1)}, s32[4]{0:T(128)}, u32[]{:S(2)}) copy-start(s32[4]{0:T(128)} %live_ref.1) | copy-start | bytes 52

commit v3 on v2

--- a/solution.py
+++ b/solution.py
@@ -172,7 +172,7 @@
             out_ref[block * count + i, LSE:TEXT] = row.astype(BF)
 
 
-def text_kernel(pair_ref, live_ref, q_ref, back_ref, out_ref):
+def text_kernel(pair_ref, live_ref, q_ref, back_ref, out_hbm, out_ref, sems):
     live = live_ref[pair_ref[0]]
     text = [
         back_ref[:, TEXT + 8 * i : TEXT + 8 * i + 8].astype(F32).reshape(TXT, HD).astype(BF) for i in range(4)
@@ -180,6 +180,7 @@
     rows = q_ref.shape[1]
     kept = lax.broadcasted_iota(jnp.int32, (rows, TXT), 1) < live
     low = lax.broadcasted_iota(jnp.int32, (8, HD), 1) < PIECE
+    stores = []
     for side in range(2):
         for head in range(2):
             owners = sorted((m for m in range(GROUP) if duty(m)[:2] == (side, head)), key=lambda m: duty(m)[3])
@@ -199,6 +200,10 @@
             acc = jnp.dot(p.astype(BF), text[2 + head], preferred_element_type=F32)
             acc += image * jnp.concatenate([back_ref[m, :PIECE] for m in owners], axis=0).astype(F32)
             out_ref[side, :, cols] = (acc / total).astype(BF)
+        stores.append(pltpu.make_async_copy(out_ref.at[side], out_hbm.at[side], sems.at[side]))
+        stores[-1].start()
+    for store in stores:
+        store.wait()
 
 
 def local(
@@ -239,7 +244,9 @@
     own = spread(image)
 
     near = call(near_kernel, (term, far), [shape(feats, text_rows + 2 * cap_cols)])
-    ring = [near] + [shifted(near, "tp", X, 2, step) for step in range(1, X)]
+    ring = [near]
+    for step in range(1, X):
+        ring.append(shifted(near, "tp", X, 2, step))
     sends = call(
         joint_kernel,
         (pos, *ring, llama_residual.T, w_kv),
@@ -248,7 +255,9 @@
         mib=8,
         scratch_shapes=[pltpu.VMEM((feats, text_rows), BF)],
     )
-    parts = [sends[0]] + [shifted(sends[step], "seq", Z_HI, GROUP, step) for step in range(1, Z_HI)]
+    parts = [sends[0]]
+    for step in range(1, Z_HI):
+        parts.append(shifted(sends[step], "seq", Z_HI, GROUP, step))
     own = after(own, sends[0])
     other = lax.ppermute(own, "seq", [(i, i ^ 1) for i in range(Z_HI * GROUP)])
     part = call(part_kernel, parts, [shape(GROUP, TXT // GROUP, kv_cols)])
@@ -256,7 +265,14 @@
     o = call(image_kernel, (own, other), [shape(GROUP, TEXT, HD)], mib=32)
     back = call(sum_kernel, (after(part, o), o), [shape(GROUP, BACK, HD)])
     back = spread(back)
-    return call(text_kernel, (pos[2:], prompt_length, image_query, back), [shape(*image_query.shape)], scalars=2)
+    return call(
+        text_kernel,
+        (pos[2:], prompt_length, image_query, back),
+        [shape(*image_query.shape)],
+        scalars=2,
+        hbm_outs=1,
+        scratch_shapes=[pltpu.VMEM(image_query.shape, BF), pltpu.SemaphoreType.DMA((image_query.shape[0],))],
+    )
 
 
 def solution(mesh):

time: 122 us -> 122 us (level)
  no operation moved by 1% of the time
where the time goes in v3:
time: 122 us; the launch traced here: 121 us
  starting transfers between devices  49.7 us (41%)
  waiting for transfers between devices  34.9 us (29%)
  blocking collectives  18.3 us (15%)
  Pallas kernels  15.3 us (13%)
  local copies, waits for them, and re-layouts  2.88 us (2%)
    ppermute x6, starting transfers between devices, shifted(): return lax.ppermute(value, axis, [(i, to(i)) for i in range(size)])  27.3 us
    ppermute x1, waiting for transfers between devices, local(): far = lax.ppermute(term, 'tp', [(t, t ^ 1) for t in range(2 * X)])  25.6 us
    all_to_all x1, blocking collectives, spread(): return lax.all_to_all(value, 'seq', 0, 0, axis_index_groups=groups)  18.3 us
    all_to_all x2, starting transfers between devices, spread(): return lax.all_to_all(value, 'seq', 0, 0, axis_index_groups=groups)  17 us
    pallas_call x7, Pallas kernels, call(): pl.pallas_call(kernel, in_specs=[smem] * scalars + [far] * hbm + [vmem] *...  15.3 us
    ppermute x6, waiting for transfers between devices, shifted(): return lax.ppermute(value, axis, [(i, to(i)) for i in range(size)])  9.24 us
    ppermute x1, starting transfers between devices, local(): other = lax.ppermute(own, 'seq', [(i, i ^ 1) for i in range(Z_HI * GROUP)])  3.18 us
    unnamed x11, local copies, waits for them, and re-layouts  2.88 us
  transfers between devices with their start and end apart: 10, of which 5 were waited for; matrix products, arithmetic and copies ran while one was open for 2% of the time, Pallas kernels for 8%

profile of v3, /device:TPU:1, one launch (start us, length us, event | category | flops | bytes accessed | tf_op | source)
XLA Modules:
  0.0 121.3 jit_solution(9519733641519107260)
XLA Ops:
  0.0 3.0 %shard_map.91 = (bf16[16,320,128]{2,1,0:T(8,128)(2,1)}, bf16[64,832]{1,0:T(8,128)(2,1)}) custom-call(bf16[2,256,256]{2,1,0:T(8,128)(2,1)} %k_hbm.1, bf16[2,256,256]{2,1,0:T(8,128)(2,1)} %v_hbm.1, bf16[2,256,256]{2,1,0:T(8,128)(2,1)} %q_ref.1, bf16[512,512]{1,0:T(8,128)(2,1)} %ctx_hbm.1, bf16[64,512]{1,0:T(8,128)(2,1)} %bitcast.10, bf16[64,320]{1,0:T(8,128)(2,1)} %cap_hbm.1), custom_call_target="tpu_custom_call" | custom-call | tf_op jit(solution)/shard_map/pallas_call | solution.py:49
  3.0 0.0 copy-start.1
  3.1 11.1 %all-to-all-start.1 = ((bf16[16,320,128]{2,1,0:T(8,128)(2,1)}), bf16[16,320,128]{2,1,0:T(8,128)(2,1)}, u32[]{:S(2)}, u32[]{:S(2)}) async-start(bf16[16,320,128]{2,1,0:T(8,128)(2,1)} %get-tuple-element.18), calls=%async_computation.1 | async-start | bytes 2621440 | tf_op jit(solution)/shard_map/all_to_all | solution.py:26
  14.2 2.1 %collective-permute-start = (bf16[64,832]{1,0:T(8,128)(2,1)S(1)}, bf16[64,832]{1,0:T(8,128)(2,1)S(1)}, u32[]{:S(2)}, u32[]{:S(2)}) collective-permute-start(bf16[64,832]{1,0:T(8,128)(2,1)S(1)} %copy-done.1), channel_id=1, source_target_pairs={{0,64},{64,0},{128,192},{192,128},{256,320},{320,256},{384,448},{4... | collective-permute-start | bytes 319496 | tf_op jit(solution)/shard_map/ppermute | solution.py:243
  16.3 25.6 %collective-permute-done.far_ref = bf16[64,832]{1,0:T(8,128)(2,1)S(1)} collective-permute-done((bf16[64,832]{1,0:T(8,128)(2,1)S(1)}, bf16[64,832]{1,0:T(8,128)(2,1)S(1)}, u32[]{:S(2)}, u32[]{:S(2)}) %collective-permute-start) | collective-permute-done | bytes 106528 | tf_op jit(solution)/shard_map/ppermute | solution.py:243
  41.9 0.1 shard_map.92.n0
  42.0 4.4 %collective-permute-start.3 = (bf16[64,1152]{1,0:T(8,128)(2,1)S(1)}, bf16[64,1152]{1,0:T(8,128)(2,1)S(1)}, u32[]{:S(2)}, u32[]{:S(2)}) collective-permute-start(bf16[64,1152]{1,0:T(8,128)(2,1)S(1)} %shard_map.92.n0), channel_id=1, source_target_pairs={{0,384},{64,448},{128,0},{192,64},{256,128},{320,192},{384,256},{4... | collective-permute-start | bytes 442376 | tf_op jit(solution)/shard_map/ppermute | solution.py:32
  46.4 2.4 %collective-permute-start.2 = (bf16[64,1152]{1,0:T(8,128)(2,1)S(1)}, bf16[64,1152]{1,0:T(8,128)(2,1)S(1)}, u32[]{:S(2)}, u32[]{:S(2)}) collective-permute-start(bf16[64,1152]{1,0:T(8,128)(2,1)S(1)} %shard_map.92.n0), channel_id=1, source_target_pairs={{0,256},{64,320},{128,384},{192,448},{256,0},{320,64},{384,128},{4... | collective-permute-start | bytes 442376 | tf_op jit(solution)/shard_map/ppermute | solution.py:32
  48.8 2.5 %collective-permute-start.1 = (bf16[64,1152]{1,0:T(8,128)(2,1)S(1)}, bf16[64,1152]{1,0:T(8,128)(2,1)S(1)}, u32[]{:S(2)}, u32[]{:S(2)}) collective-permute-start(bf16[64,1152]{1,0:T(8,128)(2,1)S(1)} %shard_map.92.n0), channel_id=1, source_target_pairs={{0,128},{64,192},{128,256},{192,320},{256,384},{320,448},{384,0},{... | collective-permute-start | bytes 442376 | tf_op jit(solution)/shard_map/ppermute | solution.py:32
  51.4 0.0 copy-start.2
  51.4 2.2 %copy.10 = bf16[320,8,2,256]{3,1,2,0:T(8,128)(2,1)S(1)} copy(bf16[320,8,2,256]{3,2,1,0:T(2,128)(2,1)} %bitcast.9) | data formatting | bytes 5242880
  53.6 0.1 pad_add_fusion.pos_ref
  53.7 0.0 collective-permute-done.3.n3
  53.7 0.5 collective-permute-done.2.n2
  54.2 3.9 %collective-permute-done.1.n1 = bf16[64,1152]{1,0:T(8,128)(2,1)S(1)} collective-permute-done((bf16[64,1152]{1,0:T(8,128)(2,1)S(1)}, bf16[64,1152]{1,0:T(8,128)(2,1)S(1)}, u32[]{:S(2)}, u32[]{:S(2)}) %collective-permute-start.1) | collective-permute-done | bytes 147488 | tf_op jit(solution)/shard_map/ppermute | solution.py:32
  58.0 1.2 shard_map.93
  59.3 0.0 copy-start.4
  59.3 0.6 copy-done.4
  59.9 0.0 all-to-all-done.1.own_ref
  59.9 3.2 %collective-permute-start.7 = (bf16[16,320,128]{2,1,0:T(8,128)(2,1)}, bf16[16,320,128]{2,1,0:T(8,128)(2,1)S(1)}, u32[]{:S(2)}, u32[]{:S(2)}) collective-permute-start(bf16[16,320,128]{2,1,0:T(8,128)(2,1)} %all-to-all-done.1.own_ref), channel_id=1, source_target_pairs={{0,1},{1,0},{2,3},{3,2},{4,5},{5,4},{6,7},{7,6},{8,9},{9,8},{10,11... | collective-permute-start | bytes 3932168 | tf_op jit(solution)/shard_map/ppermute | solution.py:262
  63.1 5.8 %collective-permute-start.4 = (bf16[64,640]{1,0:T(8,128)(2,1)}, bf16[64,640]{1,0:T(8,128)(2,1)S(1)}, u32[]{:S(2)}, u32[]{:S(2)}) collective-permute-start(bf16[64,640]{1,0:T(8,128)(2,1)} %copy-done.4), channel_id=1, source_target_pairs={{0,16},{1,17},{2,18},{3,19},{4,20},{5,21},{6,22},{7,23},{8,24},{9,... | collective-permute-start | bytes 245768 | tf_op jit(solution)/shard_map/ppermute | solution.py:32
  68.9 8.8 %collective-permute-start.5 = (bf16[64,640]{1,0:T(8,128)(2,1)S(1)}, bf16[64,640]{1,0:T(8,128)(2,1)S(1)}, u32[]{:S(2)}, u32[]{:S(2)}) collective-permute-start(bf16[64,640]{1,0:T(8,128)(2,1)S(1)} %get-tuple-element.16), channel_id=1, source_target_pairs={{0,32},{1,33},{2,34},{3,35},{4,36},{5,37},{6,38},{7,39},{8,40},{9,... | collective-permute-start | bytes 245768 | tf_op jit(solution)/shard_map/ppermute | solution.py:32
  77.7 3.4 %collective-permute-start.6 = (bf16[64,640]{1,0:T(8,128)(2,1)S(1)}, bf16[64,640]{1,0:T(8,128)(2,1)S(1)}, u32[]{:S(2)}, u32[]{:S(2)}) collective-permute-start(bf16[64,640]{1,0:T(8,128)(2,1)S(1)} %get-tuple-element.17), channel_id=1, source_target_pairs={{0,48},{1,49},{2,50},{3,51},{4,52},{5,53},{6,54},{7,55},{8,56},{9,... | collective-permute-start | bytes 245768 | tf_op jit(solution)/shard_map/ppermute | solution.py:32
  81.1 0.0 collective-permute-done.4.g1
  81.1 2.7 %collective-permute-done.5.g2 = bf16[64,640]{1,0:T(8,128)(2,1)S(1)} collective-permute-done((bf16[64,640]{1,0:T(8,128)(2,1)S(1)}, bf16[64,640]{1,0:T(8,128)(2,1)S(1)}, u32[]{:S(2)}, u32[]{:S(2)}) %collective-permute-start.5) | collective-permute-done | bytes 81952 | tf_op jit(solution)/shard_map/ppermute | solution.py:32
  83.9 2.2 %collective-permute-done.6.g3 = bf16[64,640]{1,0:T(8,128)(2,1)S(1)} collective-permute-done((bf16[64,640]{1,0:T(8,128)(2,1)S(1)}, bf16[64,640]{1,0:T(8,128)(2,1)S(1)}, u32[]{:S(2)}, u32[]{:S(2)}) %collective-permute-start.6) | collective-permute-done | bytes 81952 | tf_op jit(solution)/shard_map/ppermute | solution.py:32
  86.0 1.0 shard_map.94
  87.0 5.9 %all-to-all-start = ((bf16[16,8,512]{2,1,0:T(8,128)(2,1)}), bf16[16,8,512]{2,1,0:T(8,128)(2,1)S(1)}, u32[]{:S(2)}, u32[]{:S(2)}) async-start(bf16[16,8,512]{2,1,0:T(8,128)(2,1)} %shard_map.94), calls=%async_computation | async-start | bytes 262144 | tf_op jit(solution)/shard_map/all_to_all | solution.py:26
  92.9 7.3 %shard_map.95.o_ref = bf16[16,72,128]{2,1,0:T(8,128)(2,1)S(1)} custom-call(bf16[16,320,128]{2,1,0:T(8,128)(2,1)} %all-to-all-done.1.own_ref, bf16[16,320,128]{2,1,0:T(8,128)(2,1)S(1)} %collective-permute-done.7.other_ref), custom_call_target="tpu_custom_call" | custom-call | tf_op jit(solution)/shard_map/pallas_call | solution.py:49
  100.2 0.0 all-to-all-done.part_ref
  100.3 18.3 %all_to_all.15.back_ref = bf16[16,104,128]{2,1,0:T(8,128)(2,1)S(1)} all-to-all(bf16[16,104,128]{2,1,0:T(8,128)(2,1)S(1)} %shard_map.96), channel_id=1, replica_groups={{0,1,2,3,4,5,6,7,8,9,10,11,12,13,14,15},{16,17,18,19,20,21,22,23,24,25,..., dimensions={0} | all-to-all | bytes 851968 | tf_op jit(solution)/shard_map/all_to_all | solution.py:26
  118.6 2.7 %shard_map.97 = bf16[2,256,256]{2,1,0:T(8,128)(2,1)} custom-call(s32[1]{0:T(128)} %bitcast.pair_ref, s32[4]{0:T(128)S(1)} %copy-done.3, bf16[2,256,256]{2,1,0:T(8,128)(2,1)S(1)} %copy-done, bf16[16,104,128]{2,1,0:T(8,128)(2,1)S(1)} %all_to_all.15.back_ref), custom_call_target="tpu_custom_call" | custom-call | tf_op jit(solution)/shard_map/pallas_call | solution.py:49
  (8 shorter events, 0.1 us)
Async XLA Ops:
  3.0 11.1 %copy-start.1 = (bf16[64,832]{1,0:T(8,128)(2,1)S(1)}, bf16[64,832]{1,0:T(8,128)(2,1)}, u32[]{:S(2)}) copy-start(bf16[64,832]{1,0:T(8,128)(2,1)} %get-tuple-element.13.own_ref) | copy-start | bytes 319492
  3.1 56.8 %all-to-all-start.1 = ((bf16[16,320,128]{2,1,0:T(8,128)(2,1)}), bf16[16,320,128]{2,1,0:T(8,128)(2,1)}, u32[]{:S(2)}, u32[]{:S(2)}) async-start(bf16[16,320,128]{2,1,0:T(8,128)(2,1)} %get-tuple-element.18), calls=%async_computation.1 | async-start | bytes 2621440 | tf_op jit(solution)/shard_map/all_to_all | solution.py:26
  14.2 27.8 %collective-permute-start = (bf16[64,832]{1,0:T(8,128)(2,1)S(1)}, bf16[64,832]{1,0:T(8,128)(2,1)S(1)}, u32[]{:S(2)}, u32[]{:S(2)}) collective-permute-start(bf16[64,832]{1,0:T(8,128)(2,1)S(1)} %copy-done.1), channel_id=1, source_target_pairs={{0,64},{64,0},{128,192},{192,128},{256,320},{320,256},{384,448},{4... | collective-permute-start | bytes 319496 | tf_op jit(solution)/shard_map/ppermute | solution.py:243
  42.0 11.7 %collective-permute-start.3 = (bf16[64,1152]{1,0:T(8,128)(2,1)S(1)}, bf16[64,1152]{1,0:T(8,128)(2,1)S(1)}, u32[]{:S(2)}, u32[]{:S(2)}) collective-permute-start(bf16[64,1152]{1,0:T(8,128)(2,1)S(1)} %shard_map.92.n0), channel_id=1, source_target_pairs={{0,384},{64,448},{128,0},{192,64},{256,128},{320,192},{384,256},{4... | collective-permute-start | bytes 442376 | tf_op jit(solution)/shard_map/ppermute | solution.py:32
  46.4 7.8 %collective-permute-start.2 = (bf16[64,1152]{1,0:T(8,128)(2,1)S(1)}, bf16[64,1152]{1,0:T(8,128)(2,1)S(1)}, u32[]{:S(2)}, u32[]{:S(2)}) collective-permute-start(bf16[64,1152]{1,0:T(8,128)(2,1)S(1)} %shard_map.92.n0), channel_id=1, source_target_pairs={{0,256},{64,320},{128,384},{192,448},{256,0},{320,64},{384,128},{4... | collective-permute-start | bytes 442376 | tf_op jit(solution)/shard_map/ppermute | solution.py:32
  48.8 9.2 %collective-permute-start.1 = (bf16[64,1152]{1,0:T(8,128)(2,1)S(1)}, bf16[64,1152]{1,0:T(8,128)(2,1)S(1)}, u32[]{:S(2)}, u32[]{:S(2)}) collective-permute-start(bf16[64,1152]{1,0:T(8,128)(2,1)S(1)} %shard_map.92.n0), channel_id=1, source_target_pairs={{0,128},{64,192},{128,256},{192,320},{256,384},{320,448},{384,0},{... | collective-permute-start | bytes 442376 | tf_op jit(solution)/shard_map/ppermute | solution.py:32
  51.4 6.7 %copy-start.2 = (bf16[512,64]{0,1:T(8,128)(2,1)S(1)}, bf16[512,64]{0,1:T(8,128)(2,1)}, u32[]{:S(2)}) copy-start(bf16[512,64]{0,1:T(8,128)(2,1)} %param.10) | copy-start | bytes 196612
  59.3 0.6 copy-start.4
  59.9 33.0 %collective-permute-start.7 = (bf16[16,320,128]{2,1,0:T(8,128)(2,1)}, bf16[16,320,128]{2,1,0:T(8,128)(2,1)S(1)}, u32[]{:S(2)}, u32[]{:S(2)}) collective-permute-start(bf16[16,320,128]{2,1,0:T(8,128)(2,1)} %all-to-all-done.1.own_ref), channel_id=1, source_target_pairs={{0,1},{1,0},{2,3},{3,2},{4,5},{5,4},{6,7},{7,6},{8,9},{9,8},{10,11... | collective-permute-start | bytes 3932168 | tf_op jit(solution)/shard_map/ppermute | solution.py:262
  63.1 18.1 %collective-permute-start.4 = (bf16[64,640]{1,0:T(8,128)(2,1)}, bf16[64,640]{1,0:T(8,128)(2,1)S(1)}, u32[]{:S(2)}, u32[]{:S(2)}) collective-permute-start(bf16[64,640]{1,0:T(8,128)(2,1)} %copy-done.4), channel_id=1, source_target_pairs={{0,16},{1,17},{2,18},{3,19},{4,20},{5,21},{6,22},{7,23},{8,24},{9,... | collective-permute-start | bytes 245768 | tf_op jit(solution)/shard_map/ppermute | solution.py:32
  68.9 15.0 %collective-permute-start.5 = (bf16[64,640]{1,0:T(8,128)(2,1)S(1)}, bf16[64,640]{1,0:T(8,128)(2,1)S(1)}, u32[]{:S(2)}, u32[]{:S(2)}) collective-permute-start(bf16[64,640]{1,0:T(8,128)(2,1)S(1)} %get-tuple-element.16), channel_id=1, source_target_pairs={{0,32},{1,33},{2,34},{3,35},{4,36},{5,37},{6,38},{7,39},{8,40},{9,... | collective-permute-start | bytes 245768 | tf_op jit(solution)/shard_map/ppermute | solution.py:32
  77.7 8.3 %collective-permute-start.6 = (bf16[64,640]{1,0:T(8,128)(2,1)S(1)}, bf16[64,640]{1,0:T(8,128)(2,1)S(1)}, u32[]{:S(2)}, u32[]{:S(2)}) collective-permute-start(bf16[64,640]{1,0:T(8,128)(2,1)S(1)} %get-tuple-element.17), channel_id=1, source_target_pairs={{0,48},{1,49},{2,50},{3,51},{4,52},{5,53},{6,54},{7,55},{8,56},{9,... | collective-permute-start | bytes 245768 | tf_op jit(solution)/shard_map/ppermute | solution.py:32
  87.0 13.2 %all-to-all-start = ((bf16[16,8,512]{2,1,0:T(8,128)(2,1)}), bf16[16,8,512]{2,1,0:T(8,128)(2,1)S(1)}, u32[]{:S(2)}, u32[]{:S(2)}) async-start(bf16[16,8,512]{2,1,0:T(8,128)(2,1)} %shard_map.94), calls=%async_computation | async-start | bytes 262144 | tf_op jit(solution)/shard_map/all_to_all | solution.py:26
  100.2 18.4 %copy-start = (bf16[2,256,256]{2,1,0:T(8,128)(2,1)S(1)}, bf16[2,256,256]{2,1,0:T(8,128)(2,1)}, u32[]{:S(2)}) copy-start(bf16[2,256,256]{2,1,0:T(8,128)(2,1)} %q_ref.1) | copy-start | bytes 786436
  100.2 18.4 %copy-start.3 = (s32[4]{0:T(128)S(1)}, s32[4]{0:T(128)}, u32[]{:S(2)}) copy-start(s32[4]{0:T(128)} %live_ref.1) | copy-start | bytes 52

commit v4 on v3

--- a/solution.py
+++ b/solution.py
@@ -179,29 +179,31 @@
     ]
     rows = q_ref.shape[1]
     kept = lax.broadcasted_iota(jnp.int32, (rows, TXT), 1) < live
-    low = lax.broadcasted_iota(jnp.int32, (8, HD), 1) < PIECE
+    low = lax.broadcasted_iota(jnp.int32, (1, HD), 1) < PIECE
+    units = [(side, head) for side in range(2) for head in range(2)]
+    owners = [sorted((m for m in range(GROUP) if duty(m)[:2] == u), key=lambda m: duty(m)[3]) for u in units]
+    lse_rows, scores = [], []
+    for (side, head), group in zip(units, owners, strict=True):
+        tails = [back_ref[m, LSE:TEXT].astype(F32) for m in group]
+        lse = [tail[:1] + tail[1:2] + tail[2:3] for tail in tails]
+        lse_rows.append(jnp.concatenate([jnp.where(low, lse[0], lse[1]), jnp.where(low, lse[2], lse[3])], axis=1))
+        q = q_ref[side, :, head * HD : (head + 1) * HD]
+        scores.append(lax.dot_general(q, text[head], NT, preferred_element_type=F32) * SCALE)
+    columns = jnp.transpose(jnp.concatenate(lse_rows * 2, axis=0))
     stores = []
-    for side in range(2):
-        for head in range(2):
-            owners = sorted((m for m in range(GROUP) if duty(m)[:2] == (side, head)), key=lambda m: duty(m)[3])
-            cols = slice(head * HD, (head + 1) * HD)
-            s = lax.dot_general(q_ref[side, :, cols], text[head], NT, preferred_element_type=F32) * SCALE
-            s = jnp.where(kept, s, NEG)
-            lse = []
-            for m in owners:
-                tail = back_ref[m, LSE:TEXT].astype(F32)
-                lse.append(jnp.broadcast_to(tail[:1] + tail[1:2] + tail[2:3], tail.shape))
-            lse = jnp.concatenate([jnp.where(low, lse[0], lse[1]), jnp.where(low, lse[2], lse[3])], axis=1)
-            lse = jnp.transpose(lse)[:, :1]
-            top = jnp.maximum(jnp.max(s, axis=1, keepdims=True), lse)
-            p = jnp.exp(s - top)
-            image = jnp.exp(lse - top)
-            total = image + jnp.sum(p, axis=1, keepdims=True)
-            acc = jnp.dot(p.astype(BF), text[2 + head], preferred_element_type=F32)
-            acc += image * jnp.concatenate([back_ref[m, :PIECE] for m in owners], axis=0).astype(F32)
-            out_ref[side, :, cols] = (acc / total).astype(BF)
-        stores.append(pltpu.make_async_copy(out_ref.at[side], out_hbm.at[side], sems.at[side]))
-        stores[-1].start()
+    for i, ((side, head), group) in enumerate(zip(units, owners, strict=True)):
+        s = jnp.where(kept, scores[i], NEG)
+        lse = columns[:, i : i + 1]
+        top = jnp.maximum(jnp.max(s, axis=1, keepdims=True), lse)
+        p = jnp.exp(s - top)
+        image = jnp.exp(lse - top)
+        total = image + jnp.sum(p, axis=1, keepdims=True)
+        acc = jnp.dot(p.astype(BF), text[2 + head], preferred_element_type=F32)
+        acc += image * jnp.concatenate([back_ref[m, :PIECE] for m in group], axis=0).astype(F32)
+        out_ref[side, :, head * HD : (head + 1) * HD] = (acc / total).astype(BF)
+        if head:
+            stores.append(pltpu.make_async_copy(out_ref.at[side], out_hbm.at[side], sems.at[side]))
+            stores[-1].start()
     for store in stores:
         store.wait()
 

time: 122 us -> 122 us (level)
  no operation moved by 1% of the time
where the time goes in v4:
time: 122 us; the launch traced here: 121 us
  starting transfers between devices  49.7 us (41%)
  waiting for transfers between devices  34.9 us (29%)
  blocking collectives  18.3 us (15%)
  Pallas kernels  15.3 us (13%)
  local copies, waits for them, and re-layouts  2.88 us (2%)
    ppermute x6, starting transfers between devices, shifted(): return lax.ppermute(value, axis, [(i, to(i)) for i in range(size)])  27.3 us
    ppermute x1, waiting for transfers between devices, local(): far = lax.ppermute(term, 'tp', [(t, t ^ 1) for t in range(2 * X)])  25.6 us
    all_to_all x1, blocking collectives, spread(): return lax.all_to_all(value, 'seq', 0, 0, axis_index_groups=groups)  18.3 us
    all_to_all x2, starting transfers between devices, spread(): return lax.all_to_all(value, 'seq', 0, 0, axis_index_groups=groups)  17 us
    pallas_call x7, Pallas kernels, call(): pl.pallas_call(kernel, in_specs=[smem] * scalars + [far] * hbm + [vmem] *...  15.3 us
    ppermute x6, waiting for transfers between devices, shifted(): return lax.ppermute(value, axis, [(i, to(i)) for i in range(size)])  9.24 us
    ppermute x1, starting transfers between devices, local(): other = lax.ppermute(own, 'seq', [(i, i ^ 1) for i in range(Z_HI * GROUP)])  3.18 us
    unnamed x11, local copies, waits for them, and re-layouts  2.88 us
  transfers between devices with their start and end apart: 10, of which 5 were waited for; matrix products, arithmetic and copies ran while one was open for 2% of the time, Pallas kernels for 8%

profile of v4, /device:TPU:1, one launch (start us, length us, event | category | flops | bytes accessed | tf_op | source)
XLA Modules:
  0.0 121.2 jit_solution(2942386089511582884)
XLA Ops:
  0.0 3.0 %shard_map.91 = (bf16[16,320,128]{2,1,0:T(8,128)(2,1)}, bf16[64,832]{1,0:T(8,128)(2,1)}) custom-call(bf16[2,256,256]{2,1,0:T(8,128)(2,1)} %k_hbm.1, bf16[2,256,256]{2,1,0:T(8,128)(2,1)} %v_hbm.1, bf16[2,256,256]{2,1,0:T(8,128)(2,1)} %q_ref.1, bf16[512,512]{1,0:T(8,128)(2,1)} %ctx_hbm.1, bf16[64,512]{1,0:T(8,128)(2,1)} %bitcast.10, bf16[64,320]{1,0:T(8,128)(2,1)} %cap_hbm.1), custom_call_target="tpu_custom_call" | custom-call | tf_op jit(solution)/shard_map/pallas_call | solution.py:49
  3.0 0.0 copy-start.1
  3.1 11.1 %all-to-all-start.1 = ((bf16[16,320,128]{2,1,0:T(8,128)(2,1)}), bf16[16,320,128]{2,1,0:T(8,128)(2,1)}, u32[]{:S(2)}, u32[]{:S(2)}) async-start(bf16[16,320,128]{2,1,0:T(8,128)(2,1)} %get-tuple-element.18), calls=%async_computation.1 | async-start | bytes 2621440 | tf_op jit(solution)/shard_map/all_to_all | solution.py:26
  14.2 2.1 %collective-permute-start = (bf16[64,832]{1,0:T(8,128)(2,1)S(1)}, bf16[64,832]{1,0:T(8,128)(2,1)S(1)}, u32[]{:S(2)}, u32[]{:S(2)}) collective-permute-start(bf16[64,832]{1,0:T(8,128)(2,1)S(1)} %copy-done.1), channel_id=1, source_target_pairs={{0,64},{64,0},{128,192},{192,128},{256,320},{320,256},{384,448},{4... | collective-permute-start | bytes 319496 | tf_op jit(solution)/shard_map/ppermute | solution.py:245
  16.3 25.6 %collective-permute-done.far_ref = bf16[64,832]{1,0:T(8,128)(2,1)S(1)} collective-permute-done((bf16[64,832]{1,0:T(8,128)(2,1)S(1)}, bf16[64,832]{1,0:T(8,128)(2,1)S(1)}, u32[]{:S(2)}, u32[]{:S(2)}) %collective-permute-start) | collective-permute-done | bytes 106528 | tf_op jit(solution)/shard_map/ppermute | solution.py:245
  41.9 0.1 shard_map.92.n0
  42.0 4.4 %collective-permute-start.3 = (bf16[64,1152]{1,0:T(8,128)(2,1)S(1)}, bf16[64,1152]{1,0:T(8,128)(2,1)S(1)}, u32[]{:S(2)}, u32[]{:S(2)}) collective-permute-start(bf16[64,1152]{1,0:T(8,128)(2,1)S(1)} %shard_map.92.n0), channel_id=1, source_target_pairs={{0,384},{64,448},{128,0},{192,64},{256,128},{320,192},{384,256},{4... | collective-permute-start | bytes 442376 | tf_op jit(solution)/shard_map/ppermute | solution.py:32
  46.4 2.4 %collective-permute-start.2 = (bf16[64,1152]{1,0:T(8,128)(2,1)S(1)}, bf16[64,1152]{1,0:T(8,128)(2,1)S(1)}, u32[]{:S(2)}, u32[]{:S(2)}) collective-permute-start(bf16[64,1152]{1,0:T(8,128)(2,1)S(1)} %shard_map.92.n0), channel_id=1, source_target_pairs={{0,256},{64,320},{128,384},{192,448},{256,0},{320,64},{384,128},{4... | collective-permute-start | bytes 442376 | tf_op jit(solution)/shard_map/ppermute | solution.py:32
  48.8 2.5 %collective-permute-start.1 = (bf16[64,1152]{1,0:T(8,128)(2,1)S(1)}, bf16[64,1152]{1,0:T(8,128)(2,1)S(1)}, u32[]{:S(2)}, u32[]{:S(2)}) collective-permute-start(bf16[64,1152]{1,0:T(8,128)(2,1)S(1)} %shard_map.92.n0), channel_id=1, source_target_pairs={{0,128},{64,192},{128,256},{192,320},{256,384},{320,448},{384,0},{... | collective-permute-start | bytes 442376 | tf_op jit(solution)/shard_map/ppermute | solution.py:32
  51.4 0.0 copy-start.2
  51.4 2.2 %copy.10 = bf16[320,8,2,256]{3,1,2,0:T(8,128)(2,1)S(1)} copy(bf16[320,8,2,256]{3,2,1,0:T(2,128)(2,1)} %bitcast.9) | data formatting | bytes 5242880
  53.6 0.1 pad_add_fusion.pos_ref
  53.7 0.0 collective-permute-done.3.n3
  53.7 0.5 collective-permute-done.2.n2
  54.2 3.9 %collective-permute-done.1.n1 = bf16[64,1152]{1,0:T(8,128)(2,1)S(1)} collective-permute-done((bf16[64,1152]{1,0:T(8,128)(2,1)S(1)}, bf16[64,1152]{1,0:T(8,128)(2,1)S(1)}, u32[]{:S(2)}, u32[]{:S(2)}) %collective-permute-start.1) | collective-permute-done | bytes 147488 | tf_op jit(solution)/shard_map/ppermute | solution.py:32
  58.0 1.2 shard_map.93
  59.3 0.0 copy-start.4
  59.3 0.6 copy-done.4
  59.9 0.0 all-to-all-done.1.own_ref
  59.9 3.2 %collective-permute-start.7 = (bf16[16,320,128]{2,1,0:T(8,128)(2,1)}, bf16[16,320,128]{2,1,0:T(8,128)(2,1)S(1)}, u32[]{:S(2)}, u32[]{:S(2)}) collective-permute-start(bf16[16,320,128]{2,1,0:T(8,128)(2,1)} %all-to-all-done.1.own_ref), channel_id=1, source_target_pairs={{0,1},{1,0},{2,3},{3,2},{4,5},{5,4},{6,7},{7,6},{8,9},{9,8},{10,11... | collective-permute-start | bytes 3932168 | tf_op jit(solution)/shard_map/ppermute | solution.py:264
  63.1 5.8 %collective-permute-start.4 = (bf16[64,640]{1,0:T(8,128)(2,1)}, bf16[64,640]{1,0:T(8,128)(2,1)S(1)}, u32[]{:S(2)}, u32[]{:S(2)}) collective-permute-start(bf16[64,640]{1,0:T(8,128)(2,1)} %copy-done.4), channel_id=1, source_target_pairs={{0,16},{1,17},{2,18},{3,19},{4,20},{5,21},{6,22},{7,23},{8,24},{9,... | collective-permute-start | bytes 245768 | tf_op jit(solution)/shard_map/ppermute | solution.py:32
  68.9 8.8 %collective-permute-start.5 = (bf16[64,640]{1,0:T(8,128)(2,1)S(1)}, bf16[64,640]{1,0:T(8,128)(2,1)S(1)}, u32[]{:S(2)}, u32[]{:S(2)}) collective-permute-start(bf16[64,640]{1,0:T(8,128)(2,1)S(1)} %get-tuple-element.16), channel_id=1, source_target_pairs={{0,32},{1,33},{2,34},{3,35},{4,36},{5,37},{6,38},{7,39},{8,40},{9,... | collective-permute-start | bytes 245768 | tf_op jit(solution)/shard_map/ppermute | solution.py:32
  77.7 3.4 %collective-permute-start.6 = (bf16[64,640]{1,0:T(8,128)(2,1)S(1)}, bf16[64,640]{1,0:T(8,128)(2,1)S(1)}, u32[]{:S(2)}, u32[]{:S(2)}) collective-permute-start(bf16[64,640]{1,0:T(8,128)(2,1)S(1)} %get-tuple-element.17), channel_id=1, source_target_pairs={{0,48},{1,49},{2,50},{3,51},{4,52},{5,53},{6,54},{7,55},{8,56},{9,... | collective-permute-start | bytes 245768 | tf_op jit(solution)/shard_map/ppermute | solution.py:32
  81.1 0.0 collective-permute-done.4.g1
  81.1 2.7 %collective-permute-done.5.g2 = bf16[64,640]{1,0:T(8,128)(2,1)S(1)} collective-permute-done((bf16[64,640]{1,0:T(8,128)(2,1)S(1)}, bf16[64,640]{1,0:T(8,128)(2,1)S(1)}, u32[]{:S(2)}, u32[]{:S(2)}) %collective-permute-start.5) | collective-permute-done | bytes 81952 | tf_op jit(solution)/shard_map/ppermute | solution.py:32
  83.9 2.2 %collective-permute-done.6.g3 = bf16[64,640]{1,0:T(8,128)(2,1)S(1)} collective-permute-done((bf16[64,640]{1,0:T(8,128)(2,1)S(1)}, bf16[64,640]{1,0:T(8,128)(2,1)S(1)}, u32[]{:S(2)}, u32[]{:S(2)}) %collective-permute-start.6) | collective-permute-done | bytes 81952 | tf_op jit(solution)/shard_map/ppermute | solution.py:32
  86.0 1.0 shard_map.94
  87.0 5.9 %all-to-all-start = ((bf16[16,8,512]{2,1,0:T(8,128)(2,1)}), bf16[16,8,512]{2,1,0:T(8,128)(2,1)S(1)}, u32[]{:S(2)}, u32[]{:S(2)}) async-start(bf16[16,8,512]{2,1,0:T(8,128)(2,1)} %shard_map.94), calls=%async_computation | async-start | bytes 262144 | tf_op jit(solution)/shard_map/all_to_all | solution.py:26
  92.9 7.3 %shard_map.95.o_ref = bf16[16,72,128]{2,1,0:T(8,128)(2,1)S(1)} custom-call(bf16[16,320,128]{2,1,0:T(8,128)(2,1)} %all-to-all-done.1.own_ref, bf16[16,320,128]{2,1,0:T(8,128)(2,1)S(1)} %collective-permute-done.7.other_ref), custom_call_target="tpu_custom_call" | custom-call | tf_op jit(solution)/shard_map/pallas_call | solution.py:49
  100.2 0.0 all-to-all-done.part_ref
  100.3 18.3 %all_to_all.15.back_ref = bf16[16,104,128]{2,1,0:T(8,128)(2,1)S(1)} all-to-all(bf16[16,104,128]{2,1,0:T(8,128)(2,1)S(1)} %shard_map.96), channel_id=1, replica_groups={{0,1,2,3,4,5,6,7,8,9,10,11,12,13,14,15},{16,17,18,19,20,21,22,23,24,25,..., dimensions={0} | all-to-all | bytes 851968 | tf_op jit(solution)/shard_map/all_to_all | solution.py:26
  118.6 2.7 %shard_map.97 = bf16[2,256,256]{2,1,0:T(8,128)(2,1)} custom-call(s32[1]{0:T(128)} %bitcast.pair_ref, s32[4]{0:T(128)S(1)} %copy-done.3, bf16[2,256,256]{2,1,0:T(8,128)(2,1)S(1)} %copy-done, bf16[16,104,128]{2,1,0:T(8,128)(2,1)S(1)} %all_to_all.15.back_ref), custom_call_target="tpu_custom_call" | custom-call | tf_op jit(solution)/shard_map/pallas_call | solution.py:49
  (8 shorter events, 0.1 us)
Async XLA Ops:
  3.0 11.1 %copy-start.1 = (bf16[64,832]{1,0:T(8,128)(2,1)S(1)}, bf16[64,832]{1,0:T(8,128)(2,1)}, u32[]{:S(2)}) copy-start(bf16[64,832]{1,0:T(8,128)(2,1)} %get-tuple-element.13.own_ref) | copy-start | bytes 319492
  3.1 56.8 %all-to-all-start.1 = ((bf16[16,320,128]{2,1,0:T(8,128)(2,1)}), bf16[16,320,128]{2,1,0:T(8,128)(2,1)}, u32[]{:S(2)}, u32[]{:S(2)}) async-start(bf16[16,320,128]{2,1,0:T(8,128)(2,1)} %get-tuple-element.18), calls=%async_computation.1 | async-start | bytes 2621440 | tf_op jit(solution)/shard_map/all_to_all | solution.py:26
  14.2 27.8 %collective-permute-start = (bf16[64,832]{1,0:T(8,128)(2,1)S(1)}, bf16[64,832]{1,0:T(8,128)(2,1)S(1)}, u32[]{:S(2)}, u32[]{:S(2)}) collective-permute-start(bf16[64,832]{1,0:T(8,128)(2,1)S(1)} %copy-done.1), channel_id=1, source_target_pairs={{0,64},{64,0},{128,192},{192,128},{256,320},{320,256},{384,448},{4... | collective-permute-start | bytes 319496 | tf_op jit(solution)/shard_map/ppermute | solution.py:245
  42.0 11.7 %collective-permute-start.3 = (bf16[64,1152]{1,0:T(8,128)(2,1)S(1)}, bf16[64,1152]{1,0:T(8,128)(2,1)S(1)}, u32[]{:S(2)}, u32[]{:S(2)}) collective-permute-start(bf16[64,1152]{1,0:T(8,128)(2,1)S(1)} %shard_map.92.n0), channel_id=1, source_target_pairs={{0,384},{64,448},{128,0},{192,64},{256,128},{320,192},{384,256},{4... | collective-permute-start | bytes 442376 | tf_op jit(solution)/shard_map/ppermute | solution.py:32
  46.4 7.8 %collective-permute-start.2 = (bf16[64,1152]{1,0:T(8,128)(2,1)S(1)}, bf16[64,1152]{1,0:T(8,128)(2,1)S(1)}, u32[]{:S(2)}, u32[]{:S(2)}) collective-permute-start(bf16[64,1152]{1,0:T(8,128)(2,1)S(1)} %shard_map.92.n0), channel_id=1, source_target_pairs={{0,256},{64,320},{128,384},{192,448},{256,0},{320,64},{384,128},{4... | collective-permute-start | bytes 442376 | tf_op jit(solution)/shard_map/ppermute | solution.py:32
  48.8 9.2 %collective-permute-start.1 = (bf16[64,1152]{1,0:T(8,128)(2,1)S(1)}, bf16[64,1152]{1,0:T(8,128)(2,1)S(1)}, u32[]{:S(2)}, u32[]{:S(2)}) collective-permute-start(bf16[64,1152]{1,0:T(8,128)(2,1)S(1)} %shard_map.92.n0), channel_id=1, source_target_pairs={{0,128},{64,192},{128,256},{192,320},{256,384},{320,448},{384,0},{... | collective-permute-start | bytes 442376 | tf_op jit(solution)/shard_map/ppermute | solution.py:32
  51.4 6.7 %copy-start.2 = (bf16[512,64]{0,1:T(8,128)(2,1)S(1)}, bf16[512,64]{0,1:T(8,128)(2,1)}, u32[]{:S(2)}) copy-start(bf16[512,64]{0,1:T(8,128)(2,1)} %param.10) | copy-start | bytes 196612
  59.3 0.6 copy-start.4
  59.9 33.0 %collective-permute-start.7 = (bf16[16,320,128]{2,1,0:T(8,128)(2,1)}, bf16[16,320,128]{2,1,0:T(8,128)(2,1)S(1)}, u32[]{:S(2)}, u32[]{:S(2)}) collective-permute-start(bf16[16,320,128]{2,1,0:T(8,128)(2,1)} %all-to-all-done.1.own_ref), channel_id=1, source_target_pairs={{0,1},{1,0},{2,3},{3,2},{4,5},{5,4},{6,7},{7,6},{8,9},{9,8},{10,11... | collective-permute-start | bytes 3932168 | tf_op jit(solution)/shard_map/ppermute | solution.py:264
  63.1 18.1 %collective-permute-start.4 = (bf16[64,640]{1,0:T(8,128)(2,1)}, bf16[64,640]{1,0:T(8,128)(2,1)S(1)}, u32[]{:S(2)}, u32[]{:S(2)}) collective-permute-start(bf16[64,640]{1,0:T(8,128)(2,1)} %copy-done.4), channel_id=1, source_target_pairs={{0,16},{1,17},{2,18},{3,19},{4,20},{5,21},{6,22},{7,23},{8,24},{9,... | collective-permute-start | bytes 245768 | tf_op jit(solution)/shard_map/ppermute | solution.py:32
  68.9 15.0 %collective-permute-start.5 = (bf16[64,640]{1,0:T(8,128)(2,1)S(1)}, bf16[64,640]{1,0:T(8,128)(2,1)S(1)}, u32[]{:S(2)}, u32[]{:S(2)}) collective-permute-start(bf16[64,640]{1,0:T(8,128)(2,1)S(1)} %get-tuple-element.16), channel_id=1, source_target_pairs={{0,32},{1,33},{2,34},{3,35},{4,36},{5,37},{6,38},{7,39},{8,40},{9,... | collective-permute-start | bytes 245768 | tf_op jit(solution)/shard_map/ppermute | solution.py:32
  77.7 8.3 %collective-permute-start.6 = (bf16[64,640]{1,0:T(8,128)(2,1)S(1)}, bf16[64,640]{1,0:T(8,128)(2,1)S(1)}, u32[]{:S(2)}, u32[]{:S(2)}) collective-permute-start(bf16[64,640]{1,0:T(8,128)(2,1)S(1)} %get-tuple-element.17), channel_id=1, source_target_pairs={{0,48},{1,49},{2,50},{3,51},{4,52},{5,53},{6,54},{7,55},{8,56},{9,... | collective-permute-start | bytes 245768 | tf_op jit(solution)/shard_map/ppermute | solution.py:32
  87.0 13.2 %all-to-all-start = ((bf16[16,8,512]{2,1,0:T(8,128)(2,1)}), bf16[16,8,512]{2,1,0:T(8,128)(2,1)S(1)}, u32[]{:S(2)}, u32[]{:S(2)}) async-start(bf16[16,8,512]{2,1,0:T(8,128)(2,1)} %shard_map.94), calls=%async_computation | async-start | bytes 262144 | tf_op jit(solution)/shard_map/all_to_all | solution.py:26
  100.2 18.4 %copy-start = (bf16[2,256,256]{2,1,0:T(8,128)(2,1)S(1)}, bf16[2,256,256]{2,1,0:T(8,128)(2,1)}, u32[]{:S(2)}) copy-start(bf16[2,256,256]{2,1,0:T(8,128)(2,1)} %q_ref.1) | copy-start | bytes 786436
  100.2 18.4 %copy-start.3 = (s32[4]{0:T(128)S(1)}, s32[4]{0:T(128)}, u32[]{:S(2)}) copy-start(s32[4]{0:T(128)} %live_ref.1) | copy-start | bytes 52
